TPU v7x, 256 devices: a whole 4x4x8 slice. The times are simulated.
256 devices in a mesh: row: 16 (over y, z_lo), col: 8 (over x, core), tp: 2 (over z_hi).
Axes of the slice: x: 4, y: 4, z: 8 (z_hi: 2, z_lo: 4; z = z_hi * 4 + z_lo), core: 2. Of those that a mesh axis runs over, the one named last changes fastest.
Arguments:
- gram: float32 [8, 16, 128, 1, 8, 2048], P(None, 'row', 'tp', None, 'col'), may hold values from -24 to 24
- inv_factor: bfloat16 [1024, 1024], replicated, as said below
- cross_gram: bfloat16 [8, 16, 128, 1024], P(None, 'row', 'tp'), may hold values from -24 to 24
- down_rows: bfloat16 [29568, 4096], P(('row', 'tp'), 'col'), may hold values from -0.03125 to 0.03125
- removed: int32 [1024], replicated, may hold values from 0 to 29567, as said below
Outputs:
- updated: float32 [8, 16, 128, 1, 8, 2048], P(None, 'row', 'tp', None, 'col')
- rhs_next: float32 [8, 16, 128, 4096], P(None, 'row', 'tp', 'col')
Inputs may be any that keep to these rules, and one draw needn't show every extreme that they name: `inv_factor`: zero above the diagonal. `removed`: distinct ids in ascending order; among the neurons s * 924 to (s + 1) * 924 - 1 of any shard s at most 128 are listed, and one shard holds exactly 128.
All inputs are finite; a program needn't handle non-finite values.
Results may differ from a plain program's by a relative error of at most 0.0003.
Values may be sent and summed in bfloat16 or wider, within the bound.
A program may use at most 128 MiB of HBM per device.

v0:
```python
import jax
import jax.numpy as jnp
from jax import lax
from jax.sharding import PartitionSpec as P


def broadcast(block, axis, holder):
    block = jnp.where(lax.axis_index(axis) == holder, block, jnp.zeros_like(block))
    return lax.psum(block, axis)


def per_device(gram, inv_factor, cross_gram, down_rows, removed):
    highest = lax.Precision.HIGHEST
    cycles = gram.shape[0]
    half = gram.shape[2]
    col_cycles = gram.shape[3]
    block = gram.shape[5]
    rows_local = cycles * half
    panel_width = inv_factor.shape[0]
    grid = gram.reshape(rows_local, col_cycles, block)
    factor = inv_factor.astype(jnp.float32)
    head_columns = grid[:, 0, :panel_width]
    panel = broadcast(head_columns, "col", 0)
    left = jnp.dot(panel, factor.T, precision=highest, preferred_element_type=jnp.float32)
    col_count = lax.axis_size("col")
    by_cycle = left.reshape(col_cycles, col_count, half, panel_width)
    wanted = lax.dynamic_index_in_dim(by_cycle, lax.axis_index("col"), axis=1, keepdims=False)
    product = jnp.einsum(
        "rp,cwp->rcw",
        left,
        lax.all_gather(wanted, ("row", "tp"), axis=1, tiled=True),
        precision=highest,
        preferred_element_type=jnp.float32,
    )
    updated = grid - product
    shard = down_rows.shape[0]
    count_all = removed.shape[0]
    member = lax.axis_index(("row", "tp"))
    owner = removed // shard
    capacity = 4 * count_all // lax.axis_size(("row", "tp"))
    earlier = jnp.sum(owner[None, :] < owner[:, None], axis=1)
    within = jnp.arange(count_all, dtype=jnp.int32) - earlier
    own_start = jnp.sum(owner < member)
    slot_ids = jnp.clip(own_start + jnp.arange(capacity, dtype=jnp.int32), 0, count_all - 1)
    local_ids = jnp.clip(removed[slot_ids] - member * shard, 0, shard - 1)
    packed = jnp.take(down_rows, local_ids, axis=0)
    everyone = lax.all_gather(packed, ("row", "tp"), axis=0, tiled=True)
    lost_rows = jnp.take(everyone, owner * capacity + within, axis=0)
    cross = cross_gram.reshape(rows_local, cross_gram.shape[3])
    rhs = jnp.dot(cross, lost_rows, preferred_element_type=jnp.float32)
    leading = rhs[:half]
    stacked = lax.all_gather(leading, ("row", "tp"), axis=0, tiled=True)
    solved = jnp.dot(
        factor, stacked[:panel_width], precision=highest, preferred_element_type=jnp.float32
    )
    rhs_next = rhs - jnp.dot(left, solved, precision=highest, preferred_element_type=jnp.float32)
    return (updated.reshape(gram.shape), rhs_next.reshape(cycles, 1, half, rhs.shape[1]))


def solution(mesh):
    return jax.shard_map(
        per_device,
        mesh=mesh,
        in_specs=(
            P(None, "row", "tp", None, "col", None),
            P(),
            P(None, "row", "tp", None),
            P(("row", "tp"), "col"),
            P(),
        ),
        out_specs=(P(None, "row", "tp", None, "col", None), P(None, "row", "tp", "col")),
        check_vma=False,
    )
```

profile of v0, /device:TPU:24, one launch (start us, length us, event | category | flops | bytes accessed | tf_op | source)
XLA Modules:
  0.0 1071.5 jit_solution(9700904976470419357)
XLA Ops:
  8.0 0.0 copy-start
  8.0 0.0 all-gather.5.cloned.1.call-start
  8.1 1.5 convert_reduce_fusion.1
  9.5 0.7 fusion.10
  10.2 1.6 gather_fusion
  11.9 2.2 gather_fusion.1
  14.1 0.7 broadcast_select_fusion.1
  14.8 0.0 all-gather.5.cloned.1.call-update
  14.8 0.0 all-reduce.2.cloned.1.call-start
  14.9 3.4 broadcast_select_fusion
  18.3 1.8 copy.16
  20.1 0.0 all-reduce.2.cloned.1.call-update
  20.1 0.0 all-gather.7.cloned.1.call-start
  20.1 0.6 convert_reduce_fusion
  20.7 264.1 %all-gather.5.cloned.1.call-done = bf16[4096,512]{1,0:T(8,128)(2,1)} async-done(((bf16[128,512]{1,0:T(8,128)(2,1)}), bf16[4096,512]{1,0:T(8,128)(2,1)}) %all-gather.5.cloned.1.call-update) | async-done | bytes 4194320 | tf_op jit(solution)/shard_map/all_gather | solution.py:47
  284.8 7.8 gather_fusion.2
  292.7 2.3 convolution_bitcast_fusion
  295.0 0.7 slice.19
  295.6 0.0 all-gather.7.cloned.1.call-update
  295.7 0.2 all-gather.9.cloned.1.call-start
  295.9 0.0 all-reduce.2.cloned.1.call-done
  295.9 0.0 copy-done
  295.9 5.1 fusion.13
  301.0 0.0 copy-start.1
  301.0 1.3 copy-done.1
  302.3 0.7 constant_dynamic-slice_fusion
  303.1 0.0 all-gather.9.cloned.1.call-update
  303.1 6.2 copy.13
  309.3 257.5 %all-gather.7.cloned.1.call-done = f32[2048,512]{1,0:T(8,128)} async-done(((f32[64,512]{1,0:T(8,128)}), f32[2048,512]{1,0:T(8,128)}) %all-gather.7.cloned.1.call-update) | async-done | bytes 4194320 | tf_op jit(solution)/shard_map/all_gather | solution.py:52
  566.7 0.0 copy-start.2
  566.7 8.7 fusion.4
  575.4 0.0 copy-done.2
  575.4 4.5 convolution_subtract_fusion
  579.9 461.2 %all-gather.9.cloned.1.call-done = f32[1,1,2048,1024]{3,2,1,0:T(8,128)} async-done(((f32[1,1,64,1024]{3,2,1,0:T(8,128)}), f32[1,1,2048,1024]{3,2,1,0:T(8,128)}) %all-gather.9.cloned.1.call-update) | async-done | bytes 8388624 | tf_op jit(solution)/shard_map/all_gather | solution.py:31
  1041.1 16.9 %bitcast_subtract_fusion = f32[512,2048]{1,0:T(8,128)S(1)} fusion(f32[8,1,64,1,1,2048]{5,2,3,4,1,0:T(8,128)} %copy.13, f32[512,1024]{1,0:T(8,128)} %copy-done.1, f32[1,1,2048,1024]{3,2,1,0:T(8,128)} %all-gather.9.cloned.1.call-done), kind=kOutput, calls=%fused_computation.5 | convolution fusion | flops 12885950464 | bytes 18874368 | tf_op jit(solution)/shard_map/rp,cwp->rcw/dot_general | solution.py:28
  1058.0 6.3 copy.11
  (6 shorter events, 0.1 us)
Async XLA Ops:
  8.0 287.9 %copy-start = (bf16[1024,1024]{1,0:T(8,128)(2,1)S(1)}, bf16[1024,1024]{1,0:T(8,128)(2,1)}, u32[]{:S(2)}) copy-start(bf16[1024,1024]{1,0:T(8,128)(2,1)} %param.6) | copy-start | bytes 6291460
  8.0 276.8 %all-gather.5.cloned.1.call-start = ((), (), s32[]{:S(2)}) async-start(), calls=%async_computation.1 | async-start | bytes 4325376 | tf_op jit(solution)/shard_map/all_gather | solution.py:47
  14.8 281.1 %all-reduce.2.cloned.1.call-start = ((), (), s32[]{:S(2)}) async-start(), calls=%async_computation | async-start | bytes 4194304 | tf_op jit(solution)/shard_map/psum | solution.py:9
  20.1 546.6 %all-gather.7.cloned.1.call-start = ((), (), s32[]{:S(2)}) async-start(), calls=%async_computation.2 | async-start | bytes 4325376 | tf_op jit(solution)/shard_map/all_gather | solution.py:52
  295.7 745.5 %all-gather.9.cloned.1.call-start = ((), (), s32[]{:S(2)}) async-start(), calls=%async_computation.3 | async-start | bytes 8650752 | tf_op jit(solution)/shard_map/all_gather | solution.py:31
  301.0 1.3 copy-start.1
  566.7 8.7 copy-start.2
Sparse Core Ops, SparseCore 0:
  14.9 269.8 all-gather.4
  295.8 270.8 all-gather.6
  568.5 472.5 all-gather.8
Sparse Core Ops, SparseCore 1:
  20.2 75.2 all-reduce.1
where the time goes:
time: 1070 us
  waiting for transfers between devices  983 us (92%)
  matrix products  37.4 us (3%)
  local copies, waits for them, and re-layouts  28.6 us (3%)
  between operations  15.3 us (1%)
    all_gather x1, waiting for transfers between devices, per_device(): lax.all_gather(wanted, ('row', 'tp'), axis=1, tiled=True)  461 us
    all_gather x1, waiting for transfers between devices, per_device(): everyone = lax.all_gather(packed, ('row', 'tp'), axis=0, tiled=True)  264 us
    all_gather x1, waiting for transfers between devices, per_device(): stacked = lax.all_gather(leading, ('row', 'tp'), axis=0, tiled=True)  257 us
  transfers between devices with their start and end apart: 4, of which 3 were waited for; matrix products, arithmetic and copies ran while one was open for 4% of the time, Pallas kernels for 0%

commit v1 on v0

v1 whole, which is shorter than its diff:
```python
import jax
import jax.numpy as jnp
from jax import lax
from jax.experimental import pallas as pl
from jax.experimental.pallas import tpu as pltpu
from jax.sharding import PartitionSpec as P

NY, NZ, ZL = 4, 8, 4
MESH = pl.DeviceIdType.MESH
F32, BF16, I16 = jnp.float32, jnp.bfloat16, jnp.int16
NT, NN, TN = ((1,), (1,)), ((1,), (0,)), ((0,), (0,))
Z_HOPS = [("z+", -1, 2), ("z-", 1, 2), ("z+", -2, 2), ("z-", 2, 2), ("z+", -3, 2), ("z-", 3, 2), ("z+", 4, 0), ("z-", 4, 1)]
Y_HOPS = [("y+", -1, 2), ("y-", 1, 2), ("y+", 2, 0), ("y-", 2, 1)]


def plan(simple):
    found = [(0, a, 0, way, half) for way, a, half in Y_HOPS]
    found += [(0, a, b, way, half) for a in (0, -1, 1, 2) for way, b, half in Z_HOPS]
    if simple:
        return [t for t in found if t[4] != 1]
    found += [(1, 0, b, way, half) for way, b, half in Z_HOPS]
    return found + [(1, a, b, way, half) for b in (0, -1, 1, -2, 2, -3, 3, 4) for way, a, half in Y_HOPS]


def plan_y():
    return [(0, a, 0, way, half) for way, a, half in Y_HOPS]


def sender_chunk(t):
    part, a, b, way, half = t
    if way == "y+":
        return (part, {-1: 0, 2: -1}[a], b)
    if way == "y-":
        return (part, {1: 0, 2: 1}[a], b)
    if way == "z+":
        return (part, a, {-1: 0, -2: -1, -3: -2, 4: -3}[b])
    return (part, a, {1: 0, 2: 1, 3: 2, 4: 3}[b])


L_ROWS = {0: {0: (0, 32), 1: (32, 16), 2: (0, 48)}, 1: {0: (48, 32), 1: (80, 48), 2: (48, 80)}}
Y_ROWS = {0: {0: (0, 128), 1: (128, 128), 2: (0, 256)}}


def dot(a, b, dims):
    return lax.dot_general(a, b, (dims, ((), ())), preferred_element_type=F32)


def split2(v):
    hi = v.astype(BF16)
    return hi, (v - hi.astype(F32)).astype(BF16)


def iota(shape, axis):
    return lax.broadcasted_iota(jnp.int32, shape, axis)


def kernel(gram, inv, cross_h, down, removed, updated, rhs_out,
           gt, m_ref, cross, c0own, lsrc, ssrc, lall, sall, lrow, srow, rh, rl, ch, cl,
           c0all, c0full, pack, yslot, fbuf, zslot, lost, rhs0, hh, hl,
           g_sem, in_sem, o_sem, l_send, l_recv, s_send, s_recv, c_send, c_recv, x_send, x_recv,
           p_send, p_recv, y_send, y_recv):
    row, col, tp = lax.axis_index("row"), lax.axis_index("col"), lax.axis_index("tp")
    y, z = row // ZL, tp * ZL + lax.rem(row, ZL)
    xx, core = col // 2, lax.rem(col, 2)

    def slot_of(a, b):
        yy, zz = lax.rem(y + a + NY, NY), lax.rem(z + b + NZ, NZ)
        return yy * 8 + lax.rem(zz, ZL) * 2 + zz // ZL

    def device_of(a, b):
        yy, zz = lax.rem(y + a + NY, NY), lax.rem(z + b + NZ, NZ)
        return {"row": yy * ZL + lax.rem(zz, ZL), "col": col, "tp": zz // ZL}

    def at_col(c):
        return {"row": row, "col": c, "tp": tp}

    def peer_col(off):
        return lax.rem(xx + off, 4) * 2 + core

    to = {"y+": device_of(1, 0), "y-": device_of(-1, 0), "z+": device_of(0, 1), "z-": device_of(0, -1)}
    mine = slot_of(0, 0)

    def remote(src, dst, send, recv, dev):
        return pltpu.make_async_remote_copy(src_ref=src, dst_ref=dst, send_sem=send, recv_sem=recv, device_id=dev, device_id_type=MESH)

    loads = [pltpu.make_async_copy(gram.at[:, j, :], gt.at[j], g_sem.at[j]) for j in range(16)]
    c0load = pltpu.make_async_copy(
        cross_h.at[pl.ds(pl.multiple_of(16 * xx, 16), 16), pl.ds(pl.multiple_of(512 * core, 512), 512)], c0own, in_sem.at[0])
    m_load = pltpu.make_async_copy(inv, m_ref, in_sem.at[1])
    x_load = pltpu.make_async_copy(cross_h, cross, in_sem.at[2])
    c0load.start()
    for j in range(8):
        loads[j].start()
    m_load.start()
    for j in range(8, 16):
        loads[j].start()
    x_load.start()

    barrier = pltpu.get_barrier_semaphore()
    others = [device_of(a, 0) for a in (1, 2, 3)] + [device_of(0, b) for b in range(1, 8)]
    others += [at_col(lax.rem(col + off, 8)) for off in range(1, 8)]
    for dev in others:
        pl.semaphore_signal(barrier, inc=1, device_id=dev, device_id_type=MESH)
    pl.semaphore_wait(barrier, len(others))

    class Stream:
        def __init__(self, buf, send, recv, rows, moves):
            self.buf, self.send, self.recv, self.rows, self.moves = buf, send, recv, rows, moves

        def piece(self, t, slot):
            if self.rows is None:
                return self.buf.at[slot]
            start, count = self.rows[t[0]][t[4]]
            return self.buf.at[slot, pl.ds(start, count)]

        def slot(self, a, b):
            return slot_of(a, b)

    class YStream(Stream):
        def slot(self, a, b):
            return lax.rem(y + a + NY, NY)

    c_st = Stream(c0all, c_send, c_recv, None, plan(True))
    l_st = Stream(lall, l_send, l_recv, L_ROWS, plan(False))
    s_st = Stream(sall, s_send, s_recv, None, plan(True))
    y_st = YStream(lost, y_send, y_recv, Y_ROWS, plan_y())
    started = []

    def copy_of(st, i, slot):
        t = st.moves[i]
        return remote(st.piece(t, slot), st.piece(t, slot), st.send.at[i], st.recv.at[i], to[t[3]])

    def start_from(st, chunk):
        for i, t in enumerate(st.moves):
            if sender_chunk(t) == chunk:
                c = copy_of(st, i, st.slot(chunk[1], chunk[2]))
                c.start()
                started.append(c)

    def wait_for(st, chunk):
        for i, t in enumerate(st.moves):
            if t[:3] == chunk:
                copy_of(st, i, st.slot(chunk[1], chunk[2])).wait_recv()

    def many(copies):
        for c in copies:
            c.start()
        started.extend(copies)
        return copies

    c0load.wait()
    c0all[mine] = c0own[...]
    start_from(c_st, (0, 0, 0))

    def hand_out(c):
        return [remote(lsrc.at[c], lall.at[mine], x_send.at[c - 1], x_recv.at[0], at_col(c)),
                remote(ssrc.at[c], sall.at[mine], x_send.at[7 + c - 1], x_recv.at[1], at_col(c))]

    eye = iota((64, 128), 0) == iota((64, 128), 1)

    @pl.when(col == 0)
    def _():
        for j in range(8):
            loads[j].wait()
        m_load.wait()
        for first in (4, 0):
            r0 = first * 64
            parts = [split2(gt[j, r0:r0 + 256, :]) for j in range(8)]
            hi = jnp.concatenate([p[0] for p in parts], axis=1)
            lo = jnp.concatenate([p[1] for p in parts], axis=1)
            both = jnp.concatenate([hi, lo], axis=0)
            blocks = []
            for n in range(4):
                k = 256 * (n + 1)
                d = dot(both[:, :k], m_ref[256 * n:256 * n + 256, :k], NT)
                blocks.append(d[:256] + d[256:])
            top = jnp.maximum(blocks[0], -blocks[0])
            for b in blocks[1:]:
                top = jnp.maximum(top, jnp.abs(b))
            scale = jnp.maximum(jnp.max(top, axis=1, keepdims=True), 1e-30) / 32767.0
            inverse = 1.0 / scale
            for i in range(4):
                c = first + i
                rows = slice(64 * i, 64 * i + 64)
                for n in range(4):
                    q = lax.round(blocks[n][rows] * inverse[rows], lax.RoundingMethod.TO_NEAREST_EVEN)
                    q = jnp.clip(q, -32767.0, 32767.0).astype(jnp.int32).astype(I16)
                    half, lane = n // 2, 256 * (n % 2)
                    lsrc[c, 64 * half:64 * half + 64, lane:lane + 256] = q
                lanes = jnp.sum(jnp.where(eye, jnp.broadcast_to(scale[rows], (64, 128)), 0.0), axis=0, keepdims=True)
                ssrc[c] = jnp.broadcast_to(lanes, (8, 128))
            for c in ((4, 6, 5, 7) if first == 4 else (2, 3, 1)):
                for cp in hand_out(c):
                    cp.start()

    rem = removed[...]
    flat = jnp.concatenate([rem[i:i + 1, :] for i in range(8)], axis=1)

    def first_of(base):
        less = jnp.where(rem < base, 1.0, 0.0)
        return jnp.sum(jnp.sum(less, axis=1, keepdims=True), axis=0, keepdims=True).astype(jnp.int32)

    shard = down.shape[0]
    base = mine * shard
    place = jnp.where(iota((shard, 1024), 0) == flat - base, 1.0, 0.0).astype(BF16)
    order = jnp.where(iota((128, 1024), 1) - first_of(base) == iota((128, 1024), 0), 1.0, 0.0).astype(BF16)
    pick = dot(order, place, NT).astype(BF16)
    pack[...] = dot(pick, down[...], NN).astype(BF16)
    yslot[y] = pack[...]
    ph1 = many([remote(pack, yslot.at[y], p_send.at[a - 1], p_recv.at[a - 1], device_of(a, 0)) for a in (1, 2, 3)])

    def phase_f():
        for c in ph1:
            c.wait_recv()
        seg = jnp.concatenate([removed[pl.ds(2 * y + i, 1), :] for i in range(2)], axis=1)
        picks = []
        for yy in range(4):
            b = (yy * 8 + lax.rem(mine, 8)) * shard
            inside = (seg >= b) & (seg < b + shard)
            at = jnp.where(inside, iota((1, 256), 1) + 256 * y - first_of(b), -1)
            picks.append(jnp.where(iota((128, 256), 0) == at, 1.0, 0.0).astype(BF16))
        f = dot(jnp.concatenate(picks, axis=0), yslot[...].reshape(512, 512), TN).astype(BF16)
        for i in range(8):
            fbuf[i] = f[32 * i:32 * i + 32]
        zslot[z] = fbuf[z]
        return many([remote(fbuf.at[lax.rem(z + b, 8)], zslot.at[z], p_send.at[3 + b - 1], p_recv.at[3 + b - 1], device_of(0, b))
                     for b in range(1, 8)])

    def phase_r(ph2):
        for c in ph2:
            c.wait_recv()
        total = zslot[0].astype(F32)
        for i in range(1, 8):
            total = total + zslot[i].astype(F32)
        here = pl.ds(pl.multiple_of(32 * z, 32), 32)
        lost[y, here, :] = total.astype(BF16)
        return many([remote(lost.at[y, here], lost.at[y, here], p_send.at[10 + b - 1], p_recv.at[10 + b - 1], device_of(0, b))
                     for b in range(1, 8)])

    def x_peers(n, src, dst):
        return many([remote(src, dst.at[col], x_send.at[14 + 7 * n + off - 1], x_recv.at[2 + 7 * n + off - 1], at_col(peer_col(off)))
                     for off in range(1, 4)])

    def to_sibling(n, off, src, dst, slot):
        return many([remote(src, dst.at[slot], x_send.at[14 + 7 * n + 3 + off], x_recv.at[2 + 7 * n + 3 + off], at_col(col + 1 - 2 * core))])

    state = {}

    def own_rows():
        @pl.when(col == 0)
        def _():
            lall[mine] = lsrc[0]
            sall[mine] = ssrc[0]

        @pl.when(col != 0)
        def _():
            for k, dst in enumerate((lall, sall)):
                remote(dst.at[mine], dst.at[mine], x_send.at[0], x_recv.at[k], to["y+"]).wait_recv()
        for part in (0, 1):
            start_from(l_st, (part, 0, 0))
        start_from(s_st, (0, 0, 0))
        lrow[col] = lall[mine]
        srow[col] = sall[mine]
        state["xl"] = x_peers(0, lrow.at[col], lrow)
        state["xs"] = x_peers(1, srow.at[col], srow)
        state["sl"] = to_sibling(0, 0, lrow.at[col], lrow, col)
        state["ss"] = to_sibling(1, 0, srow.at[col], srow, col)

    def forward_rows(n, key, skey, buf):
        for off in range(1, 4):
            state[key][off - 1].wait_recv()
            c = lax.rem(xx - off + 4, 4) * 2 + core
            state[skey] += to_sibling(n, off, buf.at[c], buf, c)

    def dequant(q_ref, s_ref, slot):
        s = jnp.sum(jnp.where(eye, jnp.broadcast_to(s_ref[slot, 0:1, :], (64, 128)), 0.0), axis=1, keepdims=True)
        v = jnp.concatenate([q_ref[slot, 0:64, :], q_ref[slot, 64:128, :]], axis=1)
        return split2(v.astype(jnp.int32).astype(F32) * s)

    def rows_ready():
        for k in ("sl", "ss"):
            for c in state[k]:
                c.wait_recv()

        def body(c, _):
            hi, lo = dequant(lrow, srow, c)
            at = pl.ds(pl.multiple_of(64 * c, 64), 64)
            rh[at, :] = hi
            rl[at, :] = lo
            return 0
        lax.fori_loop(0, 8, body, 0)

    outs = []

    def columns(stage, a):
        yy = lax.rem(y + a + NY, NY)

        def body(g, _):
            for i in range(4):
                hi, lo = dequant(lall, sall, yy * 8 + 4 * g + i)
                ch[64 * i:64 * i + 64, :] = hi
                cl[64 * i:64 * i + 64, :] = lo
            p = dot(rh[...], ch[...], NT) + dot(rh[...], cl[...], NT) + dot(rl[...], ch[...], NT)
            for i in range(2):
                j = yy * 4 + 2 * g + i
                gt[j] = gt[j] - p[:, 128 * i:128 * i + 128]
                pltpu.make_async_copy(gt.at[j], updated.at[:, j, :], o_sem.at[stage * 4 + 2 * g + i]).start()
            return 0
        lax.fori_loop(0, 2, body, 0)

    def columns_sent():
        for stage, a in enumerate((0, -1, 1, 2)):
            yy = lax.rem(y + a + NY, NY)
            for i in range(4):
                j = yy * 4 + i
                pltpu.make_async_copy(gt.at[j], updated.at[:, j, :], o_sem.at[stage * 4 + i]).wait()

    def right_side():
        for c in state["sc"]:
            c.wait_recv()
        x_load.wait()
        for x4 in range(4):
            r = None
            for k in range(2):
                block = dot(c0full[2 * x4 + k].reshape(256, 512), lost[2 * k:2 * k + 2].reshape(512, 512), NN)
                r = block if r is None else r + block
            for m in range(16):
                rhs0[64 * m + 16 * x4:64 * m + 16 * x4 + 16, :] = r[16 * m:16 * m + 16]
        r_hi, r_lo = split2(rhs0[...])
        for n in range(4):
            k = 256 * (n + 1)
            mm = m_ref[256 * n:256 * n + 256, :k]
            hi, lo = split2(dot(mm, r_hi[:k], NN) + dot(mm, r_lo[:k], NN))
            hh[256 * n:256 * n + 256, :] = hi
            hl[256 * n:256 * n + 256, :] = lo
        rhs = dot(cross[...], lost[...].reshape(1024, 512), NN)
        rhs_out[...] = rhs - (dot(rh[...], hh[...], NN) + dot(rh[...], hl[...], NN) + dot(rl[...], hh[...], NN))

    def c0_done():
        c0full[col] = c0all[0:16]
        state["xc"] = x_peers(2, c0full.at[col], c0full)
        state["sc"] = to_sibling(2, 0, c0full.at[col], c0full, col)

    def loaded():
        @pl.when(col != 0)
        def _():
            for j in range(8):
                loads[j].wait()
            m_load.wait()
        for j in range(8, 16):
            loads[j].wait()

    def done_r():
        for c in state["ph3"]:
            c.wait_recv()
        start_from(y_st, (0, 0, 0))

    def y_one():
        for a in (-1, 1):
            wait_for(y_st, (0, a, 0))
            start_from(y_st, (0, a, 0))

    events = []
    for chunk in sorted({t[:3] for t in c_st.moves}):
        events.append((4 + 2 * (abs(chunk[1]) + abs(chunk[2])), 1, lambda chunk=chunk: (wait_for(c_st, chunk), start_from(c_st, chunk))))
    for st in (s_st, l_st):
        for chunk in sorted({t[:3] for t in st.moves}):
            events.append((10 + 5 * (abs(chunk[1]) + abs(chunk[2])), 2,
                           lambda st=st, chunk=chunk: (wait_for(st, chunk), start_from(st, chunk))))
    events.append((8.5, 0, lambda: state.update(ph2=phase_f())))
    events.append((10.5, 0, own_rows))
    events.append((14.5, 0, lambda: state.update(ph3=phase_r(state["ph2"]))))
    events.append((16.5, 0, c0_done))
    events.append((17, 0, lambda: forward_rows(1, "xs", "ss", srow)))
    events.append((19, 0, lambda: forward_rows(0, "xl", "sl", lrow)))
    events.append((19.5, 0, done_r))
    events.append((22, 0, loaded))
    events.append((22.5, 0, rows_ready))
    events.append((25.5, 0, y_one))
    events.append((26, 0, lambda: forward_rows(2, "xc", "sc", c0full)))
    events.append((31, 0, lambda: (wait_for(y_st, (0, 2, 0)), right_side())))
    events.append((32, 0, lambda: columns(0, 0)))
    events.append((37, 0, lambda: columns(1, -1)))
    events.append((38, 0, lambda: columns(2, 1)))
    events.append((45, 0, lambda: columns(3, 2)))
    events.sort(key=lambda e: (e[0], e[1]))
    for e in events:
        e[2]()
    for c in started:
        c.wait_send()
    columns_sent()

    @pl.when(col == 0)
    def _():
        for c in range(1, 8):
            for cp in hand_out(c):
                cp.wait_send()


def per_device(gram, inv_factor, cross_gram, down_rows, removed):
    vm = pl.BlockSpec(memory_space=pltpu.VMEM)
    hbm = pl.BlockSpec(memory_space=pl.ANY)
    dma = pltpu.SemaphoreType.DMA
    big, small = len(plan(False)), len(plan(True))
    v = pltpu.VMEM
    updated, rhs = pl.pallas_call(
        kernel,
        out_shape=[jax.ShapeDtypeStruct((512, 16, 128), F32), jax.ShapeDtypeStruct((512, 512), F32)],
        in_specs=[hbm, hbm, hbm, vm, vm],
        out_specs=[hbm, vm],
        scratch_shapes=[
            v((16, 512, 128), F32), v((1024, 1024), BF16), v((512, 1024), BF16), v((16, 512), BF16),
            v((8, 128, 512), I16), v((8, 8, 128), F32), v((32, 128, 512), I16), v((32, 8, 128), F32),
            v((8, 128, 512), I16), v((8, 8, 128), F32), v((512, 1024), BF16), v((512, 1024), BF16),
            v((256, 1024), BF16), v((256, 1024), BF16),
            v((32, 16, 512), BF16), v((8, 16, 16, 512), BF16), v((128, 512), BF16), v((4, 128, 512), BF16),
            v((8, 32, 512), BF16), v((8, 32, 512), BF16), v((4, 256, 512), BF16),
            v((1024, 512), F32), v((1024, 512), BF16), v((1024, 512), BF16),
            dma((16,)), dma((3,)), dma((16,)), dma((big,)), dma((big,)), dma((small,)), dma((small,)),
            dma((small,)), dma((small,)), dma((35,)), dma((23,)), dma((17,)), dma((17,)), dma((4,)), dma((4,)),
        ],
        compiler_params=pltpu.CompilerParams(collective_id=0, has_side_effects=True, vmem_limit_bytes=56 << 20),
    )(gram.reshape(512, 16, 128), inv_factor, cross_gram.reshape(512, 1024), down_rows, removed.reshape(8, 128))
    return (updated.reshape(gram.shape), rhs.reshape(8, 1, 64, 512))


def solution(mesh):
    return jax.shard_map(
        per_device,
        mesh=mesh,
        in_specs=(
            P(None, "row", "tp", None, "col", None),
            P(),
            P(None, "row", "tp", None),
            P(("row", "tp"), "col"),
            P(),
        ),
        out_specs=(P(None, "row", "tp", None, "col", None), P(None, "row", "tp", "col")),
        check_vma=False,
    )
```

time: 1070 us -> 92.3 us (0.09)
  the two profiles are of different devices: /device:TPU:24 before, /device:TPU:26 now
where the time goes in v1:
time: 92.3 us; the launch traced here: 92.2 us
  Pallas kernels  83.4 us (90%)
  local copies, waits for them, and re-layouts  8.14 us (9%)
    pallas_call x1, Pallas kernels, per_device(): pl.pallas_call(kernel, out_shape=[jax.ShapeDtypeStruct((512, 16, 128), F3...  83.4 us
    unnamed x4, local copies, waits for them, and re-layouts  8.14 us

profile of v1, /device:TPU:26, one launch (start us, length us, event | category | flops | bytes accessed | tf_op | source)
XLA Modules:
  0.0 92.2 jit_solution(394282328878609968)
XLA Ops:
  0.6 83.4 %shard_map.68 = (f32[512,16,128]{2,1,0:T(8,128)}, f32[512,512]{1,0:T(8,128)}) custom-call(f32[512,16,128]{2,1,0:T(8,128)} %bitcast.7, bf16[1024,1024]{1,0:T(8,128)(2,1)} %inv.1, bf16[512,1024]{1,0:T(8,128)(2,1)} %bitcast.9, bf16[924,512]{1,0:T(8,128)(2,1)} %down.1, s32[8,128]{1,0:T(8,128)} %bitcast.11), custom_call_target="tpu_custom_call" | custom-call | tf_op jit(solution)/shard_map/pallas_call | solution.py:406
  84.1 0.0 copy-start
  84.1 7.2 %copy.11 = f32[8,1,64,1,1,2048]{5,4,3,2,1,0:T(1,128)} copy(f32[8,1,64,1,1,2048]{5,4,3,2,1,0:T(1,128)} %bitcast.8) | data formatting | bytes 8388608
  91.2 0.0 copy-done
  91.2 1.0 %copy.12 = f32[8,1,64,512]{3,2,1,0:T(8,128)} copy(f32[8,1,64,512]{3,2,1,0:T(8,128)S(1)} %bitcast.10) | data formatting | bytes 2097152
Async XLA Ops:
  84.1 7.2 %copy-start = (f32[512,512]{1,0:T(8,128)S(1)}, f32[512,512]{1,0:T(8,128)}, u32[]{:S(2)}) copy-start(f32[512,512]{1,0:T(8,128)} %get-tuple-element.5) | copy-start | bytes 3145732

commit v2 on v1

--- a/solution.py
+++ b/solution.py
@@ -20,10 +20,6 @@
         return [t for t in found if t[4] != 1]
     found += [(1, 0, b, way, half) for way, b, half in Z_HOPS]
     return found + [(1, a, b, way, half) for b in (0, -1, 1, -2, 2, -3, 3, 4) for way, a, half in Y_HOPS]
-
-
-def plan_y():
-    return [(0, a, 0, way, half) for way, a, half in Y_HOPS]
 
 
 def sender_chunk(t):
@@ -38,7 +34,40 @@
 
 
 L_ROWS = {0: {0: (0, 32), 1: (32, 16), 2: (0, 48)}, 1: {0: (48, 32), 1: (80, 48), 2: (48, 80)}}
-Y_ROWS = {0: {0: (0, 128), 1: (128, 128), 2: (0, 256)}}
+R_LANES = {0: {0: (0, 128), 1: (128, 128), 2: (0, 256)}, 1: {0: (256, 128), 1: (384, 128), 2: (256, 256)}}
+
+
+ORDER = [
+    ("own",), ("C1",), ("S", 0, 0, -1), ("S", 0, 0, 1), ("F",), ("L", 0, -1, 0), ("L", 0, 1, 0), ("L", 1, 0, -1),
+    ("L", 1, 0, 1), ("L", 0, 0, -1), ("X",), ("L", 0, 0, 1), ("S", 0, 0, -2), ("S", 0, 0, 2), ("L", 1, -1, 0),
+    ("L", 1, 1, 0), ("S", 0, -1, 0), ("S", 0, 1, 0), ("rows",), ("C2",), ("L", 0, 2, 0), ("L", 1, 1, -1),
+    ("L", 1, -1, -1), ("L", 1, 1, 1), ("L", 1, -1, 1), ("L", 1, 2, 0), ("S", 0, 2, 0), ("L", 0, -1, -1),
+    ("L", 0, -1, 1), ("L", 1, 2, -1), ("Rsum",), ("L", 0, 1, -1), ("L", 0, 1, 1), ("L", 1, 2, 1), ("L", 1, 0, -2),
+    ("L", 1, 0, 2), ("L", 0, 0, -2), ("L", 0, 0, 2), ("S", 0, 0, -3), ("S", 0, 0, 3), ("S", 0, -1, -1),
+    ("S", 0, -1, 1), ("S", 0, 1, -1), ("S", 0, 1, 1), ("pair", 0, 2), ("R", 0, -1, 0), ("R", 0, 1, 0),
+    ("R", 1, -1, 0), ("R", 1, 1, 0), ("L", 0, 2, -1), ("L", 0, 2, 1), ("S", 0, 2, -1), ("S", 0, 2, 1), ("CX",),
+    ("L", 0, -1, -2), ("L", 0, -1, 2), ("R", 0, 0, -1), ("R", 0, 0, 1), ("R", 1, 0, -1), ("R", 1, 0, 1),
+    ("L", 1, -1, -2), ("L", 1, 1, -2), ("L", 0, 1, -2), ("L", 0, 1, 2), ("L", 1, -1, 2), ("L", 1, 1, 2),
+    ("R", 0, 2, 0), ("R", 1, 2, 0), ("L", 1, 0, -3), ("L", 1, 0, 3), ("R", 1, -1, -1), ("R", 1, 1, -1),
+    ("R", 1, -1, 1), ("R", 1, 1, 1), ("L", 0, 0, -3), ("L", 0, 0, 3), ("S", 0, 0, 4), ("pair", 0, 1), ("S", 0, -1, 2),
+    ("S", 0, -1, -2), ("S", 0, 1, 2), ("S", 0, 1, -2), ("R", 0, -1, 1), ("R", 0, -1, -1), ("L", 1, 2, -2),
+    ("R", 0, 1, 1), ("R", 0, 1, -1), ("pair", 0, -1), ("L", 0, 2, 2), ("L", 0, 2, -2), ("S", 0, 2, 2),
+    ("S", 0, 2, -2), ("L", 1, 2, 2), ("pair", -1, 2), ("L", 0, -1, 3), ("L", 0, -1, -3), ("pair", 1, 2),
+    ("R", 0, 0, 2), ("R", 0, 0, -2), ("L", 1, -1, -3), ("R", 1, 0, 2), ("R", 1, 0, -2), ("L", 1, 1, -3),
+    ("pair", 2, 2), ("L", 0, 1, 3), ("L", 0, 1, -3), ("R", 0, 2, 1), ("R", 0, 2, -1), ("L", 1, -1, 3), ("L", 1, 1, 3),
+    ("R", 1, 2, -1), ("R", 1, 2, 1), ("L", 1, 0, 4), ("L", 0, 0, 4), ("pair", 0, 0), ("S", 0, -1, 3),
+    ("S", 0, -1, -3), ("S", 0, 1, 3), ("S", 0, 1, -3), ("R", 0, -1, 2), ("R", 0, -1, -2), ("R", 0, 1, 2),
+    ("R", 0, 1, -2), ("R", 1, 1, 2), ("pair", -1, -1), ("R", 1, 1, -2), ("R", 1, -1, 2), ("R", 1, -1, -2),
+    ("L", 0, 2, 3), ("L", 0, 2, -3), ("S", 0, 2, 3), ("S", 0, 2, -3), ("pair", -1, 1), ("L", 1, 2, -3),
+    ("R", 0, 0, 3), ("L", 0, -1, 4), ("R", 1, 0, 3), ("R", 0, 0, -3), ("R", 1, 0, -3), ("L", 1, 2, 3),
+    ("pair", 1, -1), ("R", 0, 2, 2), ("L", 0, 1, 4), ("R", 0, -1, 3), ("L", 1, -1, 4), ("R", 0, 2, -2),
+    ("R", 0, 1, 3), ("S", 0, -1, 4), ("S", 0, 1, 4), ("pair", 1, 1), ("R", 0, -1, -3), ("L", 1, 1, 4),
+    ("R", 0, 1, -3), ("R", 1, 2, 2), ("R", 1, 2, -2), ("pair", 2, 1), ("L", 0, 2, 4), ("S", 0, 2, 4), ("R", 0, 0, 4),
+    ("pair", 2, -1), ("R", 1, -1, 3), ("R", 1, 1, 3), ("R", 1, 0, 4), ("R", 1, -1, -3), ("R", 1, 1, -3),
+    ("pair", -1, 0), ("R", 0, 2, 3), ("R", 0, 2, -3), ("pair", 1, 0), ("R", 0, -1, 4), ("R", 0, 1, 4), ("L", 1, 2, 4),
+    ("pair", 2, 0), ("R", 1, 2, 3), ("R", 1, -1, 4), ("R", 1, 1, 4), ("R", 1, 2, -3), ("R", 0, 2, 4), ("R", 1, 2, 4),
+    ("rhs",),
+]
 
 
 def dot(a, b, dims):
@@ -55,8 +84,8 @@
 
 
 def kernel(gram, inv, cross_h, down, removed, updated, rhs_out,
-           gt, m_ref, cross, c0own, lsrc, ssrc, lall, sall, lrow, srow, rh, rl, ch, cl,
-           c0all, c0full, pack, yslot, fbuf, zslot, lost, rhs0, hh, hl,
+           gt, pt, m_ref, cross, lsrc, ssrc, lall, sall, lrow, srow, rh, rl, ch,
+           c0nat, pack, yslot, fbuf, zslot, lost, hh, hl,
            g_sem, in_sem, o_sem, l_send, l_recv, s_send, s_recv, c_send, c_recv, x_send, x_recv,
            p_send, p_recv, y_send, y_recv):
     row, col, tp = lax.axis_index("row"), lax.axis_index("col"), lax.axis_index("tp")
@@ -83,17 +112,26 @@
     def remote(src, dst, send, recv, dev):
         return pltpu.make_async_remote_copy(src_ref=src, dst_ref=dst, send_sem=send, recv_sem=recv, device_id=dev, device_id_type=MESH)
 
-    loads = [pltpu.make_async_copy(gram.at[:, j, :], gt.at[j], g_sem.at[j]) for j in range(16)]
+    loads = [pltpu.make_async_copy(gram.at[:, j, :], gt.at[j], g_sem.at[j]) for j in range(8)]
+    def c0_part(first, count, c):
+        return c0nat.at[pl.ds(first, count), c // 2, :, pl.ds(pl.multiple_of(512 * lax.rem(c, 2), 512), 512)]
+
     c0load = pltpu.make_async_copy(
-        cross_h.at[pl.ds(pl.multiple_of(16 * xx, 16), 16), pl.ds(pl.multiple_of(512 * core, 512), 512)], c0own, in_sem.at[0])
+        cross_h.at[pl.ds(pl.multiple_of(16 * xx, 16), 16), pl.ds(pl.multiple_of(512 * core, 512), 512)],
+        c0_part(mine, 1, col).at[0], in_sem.at[0])
     m_load = pltpu.make_async_copy(inv, m_ref, in_sem.at[1])
     x_load = pltpu.make_async_copy(cross_h, cross, in_sem.at[2])
-    c0load.start()
-    for j in range(8):
-        loads[j].start()
+
+    @pl.when(y < 2)
+    def _():
+        c0load.start()
+
+
+    @pl.when(col == 0)
+    def _():
+        for j in range(8):
+            loads[j].start()
     m_load.start()
-    for j in range(8, 16):
-        loads[j].start()
     x_load.start()
 
     barrier = pltpu.get_barrier_semaphore()
@@ -116,14 +154,17 @@
         def slot(self, a, b):
             return slot_of(a, b)
 
-    class YStream(Stream):
+    class LaneStream(Stream):
+        def piece(self, t, slot):
+            start, count = self.rows[t[0]][t[4]]
+            return self.buf.at[slot, :, pl.ds(start, count)]
+
         def slot(self, a, b):
-            return lax.rem(y + a + NY, NY)
-
-    c_st = Stream(c0all, c_send, c_recv, None, plan(True))
+            return lax.rem(y + a + NY, NY) * 8 + lax.rem(z + b + NZ, NZ)
+
     l_st = Stream(lall, l_send, l_recv, L_ROWS, plan(False))
     s_st = Stream(sall, s_send, s_recv, None, plan(True))
-    y_st = YStream(lost, y_send, y_recv, Y_ROWS, plan_y())
+    r_st = LaneStream(lost, y_send, y_recv, R_LANES, plan(False))
     started = []
 
     def copy_of(st, i, slot):
@@ -148,9 +189,35 @@
         started.extend(copies)
         return copies
 
-    c0load.wait()
-    c0all[mine] = c0own[...]
-    start_from(c_st, (0, 0, 0))
+    def c0_z():
+        return [remote(c0_part(mine, 1, col), c0_part(mine, 1, col), c_send.at[b - 1], c_recv.at[b - 1], device_of(0, b))
+                for b in range(1, 8)]
+
+    def c0_y(n):
+        block = c0_part(8 * y, 8, col)
+        return [remote(block, block, c_send.at[6 + a], c_recv.at[7 + n], device_of(a, 0)) for a in (1, 2, 3)]
+
+    @pl.when(y < 2)
+    def _():
+        c0load.wait()
+        for c in c0_z():
+            c.start()
+
+    rem = removed[...]
+    flat = jnp.concatenate([rem[i:i + 1, :] for i in range(8)], axis=1)
+
+    def first_of(base):
+        less = jnp.where(rem < base, 1.0, 0.0)
+        return jnp.sum(jnp.sum(less, axis=1, keepdims=True), axis=0, keepdims=True).astype(jnp.int32)
+
+    shard = down.shape[0]
+    base = mine * shard
+    place = jnp.where(iota((shard, 1024), 0) == flat - base, 1.0, 0.0).astype(BF16)
+    order = jnp.where(iota((128, 1024), 1) - first_of(base) == iota((128, 1024), 0), 1.0, 0.0).astype(BF16)
+    pick = dot(order, place, NT).astype(BF16)
+    pack[...] = dot(pick, down[...], NN).astype(BF16)
+    yslot[y] = pack[...]
+    ph1 = many([remote(pack, yslot.at[y], p_send.at[a - 1], p_recv.at[a - 1], device_of(a, 0)) for a in (1, 2, 3)])
 
     def hand_out(c):
         return [remote(lsrc.at[c], lall.at[mine], x_send.at[c - 1], x_recv.at[0], at_col(c)),
@@ -193,22 +260,6 @@
                 for cp in hand_out(c):
                     cp.start()
 
-    rem = removed[...]
-    flat = jnp.concatenate([rem[i:i + 1, :] for i in range(8)], axis=1)
-
-    def first_of(base):
-        less = jnp.where(rem < base, 1.0, 0.0)
-        return jnp.sum(jnp.sum(less, axis=1, keepdims=True), axis=0, keepdims=True).astype(jnp.int32)
-
-    shard = down.shape[0]
-    base = mine * shard
-    place = jnp.where(iota((shard, 1024), 0) == flat - base, 1.0, 0.0).astype(BF16)
-    order = jnp.where(iota((128, 1024), 1) - first_of(base) == iota((128, 1024), 0), 1.0, 0.0).astype(BF16)
-    pick = dot(order, place, NT).astype(BF16)
-    pack[...] = dot(pick, down[...], NN).astype(BF16)
-    yslot[y] = pack[...]
-    ph1 = many([remote(pack, yslot.at[y], p_send.at[a - 1], p_recv.at[a - 1], device_of(a, 0)) for a in (1, 2, 3)])
-
     def phase_f():
         for c in ph1:
             c.wait_recv()
@@ -232,10 +283,9 @@
         total = zslot[0].astype(F32)
         for i in range(1, 8):
             total = total + zslot[i].astype(F32)
-        here = pl.ds(pl.multiple_of(32 * z, 32), 32)
-        lost[y, here, :] = total.astype(BF16)
-        return many([remote(lost.at[y, here], lost.at[y, here], p_send.at[10 + b - 1], p_recv.at[10 + b - 1], device_of(0, b))
-                     for b in range(1, 8)])
+        lost[y * 8 + z] = total.astype(BF16)
+        for part in (0, 1):
+            start_from(r_st, (part, 0, 0))
 
     def x_peers(n, src, dst):
         return many([remote(src, dst.at[col], x_send.at[14 + 7 * n + off - 1], x_recv.at[2 + 7 * n + off - 1], at_col(peer_col(off)))
@@ -292,41 +342,25 @@
 
     outs = []
 
-    def columns(stage, a):
-        yy = lax.rem(y + a + NY, NY)
-
-        def body(g, _):
-            for i in range(4):
-                hi, lo = dequant(lall, sall, yy * 8 + 4 * g + i)
-                ch[64 * i:64 * i + 64, :] = hi
-                cl[64 * i:64 * i + 64, :] = lo
-            p = dot(rh[...], ch[...], NT) + dot(rh[...], cl[...], NT) + dot(rl[...], ch[...], NT)
-            for i in range(2):
-                j = yy * 4 + 2 * g + i
-                gt[j] = gt[j] - p[:, 128 * i:128 * i + 128]
-                pltpu.make_async_copy(gt.at[j], updated.at[:, j, :], o_sem.at[stage * 4 + 2 * g + i]).start()
-            return 0
-        lax.fori_loop(0, 2, body, 0)
-
-    def columns_sent():
-        for stage, a in enumerate((0, -1, 1, 2)):
-            yy = lax.rem(y + a + NY, NY)
-            for i in range(4):
-                j = yy * 4 + i
-                pltpu.make_async_copy(gt.at[j], updated.at[:, j, :], o_sem.at[stage * 4 + i]).wait()
+    def columns(n, a, b):
+        yy, zl = lax.rem(y + a + NY, NY), lax.rem(z + b + NZ, ZL)
+        j = yy * 4 + zl
+        for i in range(2):
+            hi, lo = dequant(lall, sall, 2 * j + i)
+            ch[64 * i:64 * i + 64, :] = hi
+            ch[128 + 64 * i:192 + 64 * i, :] = lo
+        p = dot(rh[...], ch[...], NT)
+        p = p[:, :128] + p[:, 128:] + dot(rl[...], ch[:128], NT)
+        pt[j] = p
+        cp = pltpu.make_async_copy(pt.at[j], updated.at[:, j, :], o_sem.at[n])
+        cp.start()
+        outs.append(cp)
 
     def right_side():
         for c in state["sc"]:
             c.wait_recv()
         x_load.wait()
-        for x4 in range(4):
-            r = None
-            for k in range(2):
-                block = dot(c0full[2 * x4 + k].reshape(256, 512), lost[2 * k:2 * k + 2].reshape(512, 512), NN)
-                r = block if r is None else r + block
-            for m in range(16):
-                rhs0[64 * m + 16 * x4:64 * m + 16 * x4 + 16, :] = r[16 * m:16 * m + 16]
-        r_hi, r_lo = split2(rhs0[...])
+        r_hi, r_lo = split2(dot(c0nat[...].reshape(1024, 1024), lost[...].reshape(1024, 512), NN))
         for n in range(4):
             k = 256 * (n + 1)
             mm = m_ref[256 * n:256 * n + 256, :k]
@@ -336,59 +370,70 @@
         rhs = dot(cross[...], lost[...].reshape(1024, 512), NN)
         rhs_out[...] = rhs - (dot(rh[...], hh[...], NN) + dot(rh[...], hl[...], NN) + dot(rl[...], hh[...], NN))
 
+    def c0_across():
+        @pl.when(y < 2)
+        def _():
+            for c in c0_z():
+                c.wait_recv()
+
+        for n in range(2):
+            @pl.when(y == n)
+            def _():
+                for c in c0_y(n):
+                    c.start()
+
     def c0_done():
-        c0full[col] = c0all[0:16]
-        state["xc"] = x_peers(2, c0full.at[col], c0full)
-        state["sc"] = to_sibling(2, 0, c0full.at[col], c0full, col)
+        for n in range(2):
+            @pl.when(y != n)
+            def _():
+                block = c0_part(8 * n, 8, col)
+                remote(block, block, c_send.at[0], c_recv.at[7 + n], to["y+"]).wait_recv()
+        own = c0_part(0, 16, col)
+        state["xc"] = many([remote(own, own, x_send.at[28 + off - 1], x_recv.at[16 + off - 1], at_col(peer_col(off))) for off in range(1, 4)])
+        state["sc"] = many([remote(own, own, x_send.at[31], x_recv.at[19], at_col(col + 1 - 2 * core))])
+
+    def c0_forward():
+        for off in range(1, 4):
+            state["xc"][off - 1].wait_recv()
+            block = c0_part(0, 16, lax.rem(xx - off + 4, 4) * 2 + core)
+            state["sc"] += many([remote(block, block, x_send.at[31 + off], x_recv.at[19 + off], at_col(col + 1 - 2 * core))])
 
     def loaded():
         @pl.when(col != 0)
         def _():
-            for j in range(8):
-                loads[j].wait()
             m_load.wait()
-        for j in range(8, 16):
-            loads[j].wait()
-
-    def done_r():
-        for c in state["ph3"]:
-            c.wait_recv()
-        start_from(y_st, (0, 0, 0))
-
-    def y_one():
-        for a in (-1, 1):
-            wait_for(y_st, (0, a, 0))
-            start_from(y_st, (0, a, 0))
-
-    events = []
-    for chunk in sorted({t[:3] for t in c_st.moves}):
-        events.append((4 + 2 * (abs(chunk[1]) + abs(chunk[2])), 1, lambda chunk=chunk: (wait_for(c_st, chunk), start_from(c_st, chunk))))
-    for st in (s_st, l_st):
-        for chunk in sorted({t[:3] for t in st.moves}):
-            events.append((10 + 5 * (abs(chunk[1]) + abs(chunk[2])), 2,
-                           lambda st=st, chunk=chunk: (wait_for(st, chunk), start_from(st, chunk))))
-    events.append((8.5, 0, lambda: state.update(ph2=phase_f())))
-    events.append((10.5, 0, own_rows))
-    events.append((14.5, 0, lambda: state.update(ph3=phase_r(state["ph2"]))))
-    events.append((16.5, 0, c0_done))
-    events.append((17, 0, lambda: forward_rows(1, "xs", "ss", srow)))
-    events.append((19, 0, lambda: forward_rows(0, "xl", "sl", lrow)))
-    events.append((19.5, 0, done_r))
-    events.append((22, 0, loaded))
-    events.append((22.5, 0, rows_ready))
-    events.append((25.5, 0, y_one))
-    events.append((26, 0, lambda: forward_rows(2, "xc", "sc", c0full)))
-    events.append((31, 0, lambda: (wait_for(y_st, (0, 2, 0)), right_side())))
-    events.append((32, 0, lambda: columns(0, 0)))
-    events.append((37, 0, lambda: columns(1, -1)))
-    events.append((38, 0, lambda: columns(2, 1)))
-    events.append((45, 0, lambda: columns(3, 2)))
-    events.sort(key=lambda e: (e[0], e[1]))
-    for e in events:
-        e[2]()
+
+    streams = {"L": l_st, "R": r_st, "S": s_st}
+    steps = {
+        "own": own_rows,
+        "F": lambda: state.update(ph2=phase_f()),
+        "Rsum": lambda: phase_r(state["ph2"]),
+        "C1": c0_across,
+        "C2": c0_done,
+        "CX": c0_forward,
+        "X": lambda: (forward_rows(1, "xs", "ss", srow), forward_rows(0, "xl", "sl", lrow)),
+        "rows": lambda: (loaded(), rows_ready()),
+        "rhs": right_side,
+    }
+    pairs = 0
+    for event in ORDER:
+        if event[0] in streams:
+            wait_for(streams[event[0]], event[1:])
+            start_from(streams[event[0]], event[1:])
+        elif event[0] == "pair":
+            columns(pairs, event[1], event[2])
+            pairs += 1
+        else:
+            steps[event[0]]()
     for c in started:
         c.wait_send()
-    columns_sent()
+    for c in outs:
+        c.wait()
+
+    @pl.when(y < 2)
+    def _():
+        for c in c0_z() + c0_y(0):
+            c.wait_send()
 
     @pl.when(col == 0)
     def _():
@@ -409,18 +454,19 @@
         in_specs=[hbm, hbm, hbm, vm, vm],
         out_specs=[hbm, vm],
         scratch_shapes=[
-            v((16, 512, 128), F32), v((1024, 1024), BF16), v((512, 1024), BF16), v((16, 512), BF16),
+            v((8, 512, 128), F32), v((16, 512, 128), F32), v((1024, 1024), BF16), v((512, 1024), BF16),
             v((8, 128, 512), I16), v((8, 8, 128), F32), v((32, 128, 512), I16), v((32, 8, 128), F32),
             v((8, 128, 512), I16), v((8, 8, 128), F32), v((512, 1024), BF16), v((512, 1024), BF16),
-            v((256, 1024), BF16), v((256, 1024), BF16),
-            v((32, 16, 512), BF16), v((8, 16, 16, 512), BF16), v((128, 512), BF16), v((4, 128, 512), BF16),
-            v((8, 32, 512), BF16), v((8, 32, 512), BF16), v((4, 256, 512), BF16),
-            v((1024, 512), F32), v((1024, 512), BF16), v((1024, 512), BF16),
-            dma((16,)), dma((3,)), dma((16,)), dma((big,)), dma((big,)), dma((small,)), dma((small,)),
-            dma((small,)), dma((small,)), dma((35,)), dma((23,)), dma((17,)), dma((17,)), dma((4,)), dma((4,)),
+            v((256, 1024), BF16),
+            v((16, 4, 16, 1024), BF16), v((128, 512), BF16), v((4, 128, 512), BF16),
+            v((8, 32, 512), BF16), v((8, 32, 512), BF16), v((32, 32, 512), BF16),
+            v((1024, 512), BF16), v((1024, 512), BF16),
+            dma((8,)), dma((3,)), dma((16,)), dma((big,)), dma((big,)), dma((small,)), dma((small,)),
+            dma((10,)), dma((9,)), dma((35,)), dma((23,)), dma((10,)), dma((10,)), dma((big,)), dma((big,)),
         ],
         compiler_params=pltpu.CompilerParams(collective_id=0, has_side_effects=True, vmem_limit_bytes=56 << 20),
     )(gram.reshape(512, 16, 128), inv_factor, cross_gram.reshape(512, 1024), down_rows, removed.reshape(8, 128))
+    updated = gram.reshape(512, 16, 128) - updated
     return (updated.reshape(gram.shape), rhs.reshape(8, 1, 64, 512))
 
 

time: 92.3 us -> 85.1 us (0.922)
  the two profiles are of different devices: /device:TPU:26 before, /device:TPU:24 now
where the time goes in v2:
time: 85.1 us; the launch traced here: 84.6 us
  Pallas kernels  78.2 us (92%)
  other arithmetic  4.83 us (6%)
  local copies, waits for them, and re-layouts  0.98 us (1%)
    pallas_call x1, Pallas kernels, per_device(): pl.pallas_call(kernel, out_shape=[jax.ShapeDtypeStruct((512, 16, 128), F3...  78.2 us
    sub x1, other arithmetic, per_device(): updated = gram.reshape(512, 16, 128) - updated  4.83 us

profile of v2, /device:TPU:24, one launch (start us, length us, event | category | flops | bytes accessed | tf_op | source)
XLA Modules:
  0.0 84.6 jit_solution(13222124063544593107)
XLA Ops:
  0.6 0.0 copy-start
  0.6 78.2 %shard_map.68 = (f32[512,16,128]{2,1,0:T(8,128)}, f32[512,512]{1,0:T(8,128)}) custom-call(f32[512,16,128]{2,1,0:T(8,128)} %bitcast.7, bf16[1024,1024]{1,0:T(8,128)(2,1)} %inv.1, bf16[512,1024]{1,0:T(8,128)(2,1)} %bitcast.10, bf16[924,512]{1,0:T(8,128)(2,1)} %down.1, s32[8,128]{1,0:T(8,128)} %bitcast.12), custom_call_target="tpu_custom_call" | custom-call | tf_op jit(solution)/shard_map/pallas_call | solution.py:451
  78.8 0.0 copy-done
  78.8 0.0 copy-start.1
  78.8 4.8 %sub.3 = f32[512,16,128]{2,1,0:T(8,128)} subtract(f32[512,16,128]{2,1,0:T(8,128)S(1)} %bitcast.8, f32[512,16,128]{2,1,0:T(8,128)} %get-tuple-element.4) | non-fusion elementwise | flops 1048576 | bytes 12582912 | tf_op jit(solution)/shard_map/sub | solution.py:469
  83.7 0.0 copy-done.1
  83.7 1.0 %copy.10 = f32[8,1,64,512]{3,2,1,0:T(8,128)} copy(f32[8,1,64,512]{3,2,1,0:T(8,128)S(1)} %bitcast.11) | data formatting | bytes 2097152
Async XLA Ops:
  0.6 78.2 %copy-start = (f32[8,1,64,1,1,2048]{5,4,3,2,1,0:T(1,128)S(1)}, f32[8,1,64,1,1,2048]{5,4,3,2,1,0:T(1,128)}, u32[]{:S(2)}) copy-start(f32[8,1,64,1,1,2048]{5,4,3,2,1,0:T(1,128)} %param.5) | copy-start | bytes 12582916
  78.8 4.8 %copy-start.1 = (f32[512,512]{1,0:T(8,128)S(1)}, f32[512,512]{1,0:T(8,128)}, u32[]{:S(2)}) copy-start(f32[512,512]{1,0:T(8,128)} %get-tuple-element.5) | copy-start | bytes 3145732

commit v3 on v2

--- a/solution.py
+++ b/solution.py
@@ -38,35 +38,34 @@
 
 
 ORDER = [
-    ("own",), ("C1",), ("S", 0, 0, -1), ("S", 0, 0, 1), ("F",), ("L", 0, -1, 0), ("L", 0, 1, 0), ("L", 1, 0, -1),
-    ("L", 1, 0, 1), ("L", 0, 0, -1), ("X",), ("L", 0, 0, 1), ("S", 0, 0, -2), ("S", 0, 0, 2), ("L", 1, -1, 0),
-    ("L", 1, 1, 0), ("S", 0, -1, 0), ("S", 0, 1, 0), ("rows",), ("C2",), ("L", 0, 2, 0), ("L", 1, 1, -1),
-    ("L", 1, -1, -1), ("L", 1, 1, 1), ("L", 1, -1, 1), ("L", 1, 2, 0), ("S", 0, 2, 0), ("L", 0, -1, -1),
-    ("L", 0, -1, 1), ("L", 1, 2, -1), ("Rsum",), ("L", 0, 1, -1), ("L", 0, 1, 1), ("L", 1, 2, 1), ("L", 1, 0, -2),
-    ("L", 1, 0, 2), ("L", 0, 0, -2), ("L", 0, 0, 2), ("S", 0, 0, -3), ("S", 0, 0, 3), ("S", 0, -1, -1),
-    ("S", 0, -1, 1), ("S", 0, 1, -1), ("S", 0, 1, 1), ("pair", 0, 2), ("R", 0, -1, 0), ("R", 0, 1, 0),
-    ("R", 1, -1, 0), ("R", 1, 1, 0), ("L", 0, 2, -1), ("L", 0, 2, 1), ("S", 0, 2, -1), ("S", 0, 2, 1), ("CX",),
-    ("L", 0, -1, -2), ("L", 0, -1, 2), ("R", 0, 0, -1), ("R", 0, 0, 1), ("R", 1, 0, -1), ("R", 1, 0, 1),
-    ("L", 1, -1, -2), ("L", 1, 1, -2), ("L", 0, 1, -2), ("L", 0, 1, 2), ("L", 1, -1, 2), ("L", 1, 1, 2),
-    ("R", 0, 2, 0), ("R", 1, 2, 0), ("L", 1, 0, -3), ("L", 1, 0, 3), ("R", 1, -1, -1), ("R", 1, 1, -1),
-    ("R", 1, -1, 1), ("R", 1, 1, 1), ("L", 0, 0, -3), ("L", 0, 0, 3), ("S", 0, 0, 4), ("pair", 0, 1), ("S", 0, -1, 2),
-    ("S", 0, -1, -2), ("S", 0, 1, 2), ("S", 0, 1, -2), ("R", 0, -1, 1), ("R", 0, -1, -1), ("L", 1, 2, -2),
-    ("R", 0, 1, 1), ("R", 0, 1, -1), ("pair", 0, -1), ("L", 0, 2, 2), ("L", 0, 2, -2), ("S", 0, 2, 2),
-    ("S", 0, 2, -2), ("L", 1, 2, 2), ("pair", -1, 2), ("L", 0, -1, 3), ("L", 0, -1, -3), ("pair", 1, 2),
-    ("R", 0, 0, 2), ("R", 0, 0, -2), ("L", 1, -1, -3), ("R", 1, 0, 2), ("R", 1, 0, -2), ("L", 1, 1, -3),
-    ("pair", 2, 2), ("L", 0, 1, 3), ("L", 0, 1, -3), ("R", 0, 2, 1), ("R", 0, 2, -1), ("L", 1, -1, 3), ("L", 1, 1, 3),
-    ("R", 1, 2, -1), ("R", 1, 2, 1), ("L", 1, 0, 4), ("L", 0, 0, 4), ("pair", 0, 0), ("S", 0, -1, 3),
-    ("S", 0, -1, -3), ("S", 0, 1, 3), ("S", 0, 1, -3), ("R", 0, -1, 2), ("R", 0, -1, -2), ("R", 0, 1, 2),
-    ("R", 0, 1, -2), ("R", 1, 1, 2), ("pair", -1, -1), ("R", 1, 1, -2), ("R", 1, -1, 2), ("R", 1, -1, -2),
-    ("L", 0, 2, 3), ("L", 0, 2, -3), ("S", 0, 2, 3), ("S", 0, 2, -3), ("pair", -1, 1), ("L", 1, 2, -3),
-    ("R", 0, 0, 3), ("L", 0, -1, 4), ("R", 1, 0, 3), ("R", 0, 0, -3), ("R", 1, 0, -3), ("L", 1, 2, 3),
-    ("pair", 1, -1), ("R", 0, 2, 2), ("L", 0, 1, 4), ("R", 0, -1, 3), ("L", 1, -1, 4), ("R", 0, 2, -2),
-    ("R", 0, 1, 3), ("S", 0, -1, 4), ("S", 0, 1, 4), ("pair", 1, 1), ("R", 0, -1, -3), ("L", 1, 1, 4),
-    ("R", 0, 1, -3), ("R", 1, 2, 2), ("R", 1, 2, -2), ("pair", 2, 1), ("L", 0, 2, 4), ("S", 0, 2, 4), ("R", 0, 0, 4),
-    ("pair", 2, -1), ("R", 1, -1, 3), ("R", 1, 1, 3), ("R", 1, 0, 4), ("R", 1, -1, -3), ("R", 1, 1, -3),
-    ("pair", -1, 0), ("R", 0, 2, 3), ("R", 0, 2, -3), ("pair", 1, 0), ("R", 0, -1, 4), ("R", 0, 1, 4), ("L", 1, 2, 4),
-    ("pair", 2, 0), ("R", 1, 2, 3), ("R", 1, -1, 4), ("R", 1, 1, 4), ("R", 1, 2, -3), ("R", 0, 2, 4), ("R", 1, 2, 4),
-    ("rhs",),
+    ("own",), ("S", 0, 0, -1), ("S", 0, 0, 1), ("C1",), ("L", 1, 0, -1), ("L", 1, 0, 1), ("F",), ("L", 0, 0, -1),
+    ("X",), ("L", 0, 0, 1), ("S", 0, 0, -2), ("L", 0, -1, 0), ("S", 0, 0, 2), ("L", 0, 1, 0), ("L", 1, -1, 0),
+    ("L", 1, 1, 0), ("S", 0, -1, 0), ("S", 0, 1, 0), ("rows",), ("L", 1, 0, -2), ("L", 1, 0, 2), ("C2",),
+    ("L", 1, -1, -1), ("L", 1, 1, -1), ("L", 1, -1, 1), ("L", 1, 1, 1), ("L", 0, 2, 0), ("L", 1, 2, 0),
+    ("S", 0, 2, 0), ("L", 0, 0, -2), ("S", 0, 0, -3), ("L", 0, 0, 2), ("pair", 0, 2), ("Rsum",), ("L", 0, -1, -1),
+    ("L", 0, -1, 1), ("L", 1, 1, -2), ("S", 0, 0, 3), ("L", 1, -1, -2), ("L", 0, 1, -1), ("S", 0, -1, -1),
+    ("S", 0, 1, -1), ("L", 0, 1, 1), ("S", 0, -1, 1), ("S", 0, 1, 1), ("L", 1, 1, 2), ("L", 1, -1, 2),
+    ("L", 1, 2, -1), ("L", 1, 0, -3), ("L", 1, 0, 3), ("CX",), ("R", 0, -1, 0), ("L", 1, 2, 1), ("L", 0, 2, -1),
+    ("R", 1, -1, 0), ("S", 0, 2, -1), ("L", 0, 2, 1), ("S", 0, 2, 1), ("R", 0, 1, 0), ("R", 1, 1, 0), ("L", 0, 0, -3),
+    ("pair", 0, 1), ("S", 0, 0, 4), ("L", 0, 0, 3), ("R", 0, 0, -1), ("R", 0, 0, 1), ("L", 1, 2, -2), ("R", 1, 0, -1),
+    ("R", 1, 0, 1), ("pair", 0, -1), ("L", 1, 2, 2), ("L", 0, -1, -2), ("L", 0, -1, 2), ("L", 1, -1, -3),
+    ("L", 0, 1, -2), ("S", 0, -1, -2), ("L", 0, 1, 2), ("S", 0, 1, -2), ("S", 0, -1, 2), ("S", 0, 1, 2),
+    ("pair", -1, 2), ("L", 1, 1, -3), ("R", 0, -1, -1), ("pair", 1, 2), ("L", 1, 0, 4), ("L", 1, -1, 3),
+    ("R", 0, -1, 1), ("CW",), ("R", 1, -1, -1), ("L", 1, 1, 3), ("L", 0, 2, -2), ("S", 0, 2, -2), ("R", 1, -1, 1),
+    ("R", 0, 2, 0), ("R", 1, 2, 0), ("R", 0, 1, -1), ("L", 0, 2, 2), ("S", 0, 2, 2), ("pair", 2, 2), ("R", 1, 1, -1),
+    ("R", 0, 1, 1), ("R", 1, 1, 1), ("L", 0, 0, 4), ("R", 0, 0, -2), ("R", 0, 0, 2), ("pair", 0, 0), ("R", 1, 0, -2),
+    ("R", 1, 0, 2), ("L", 1, 2, -3), ("L", 0, -1, -3), ("L", 0, -1, 3), ("L", 0, 1, -3), ("S", 0, -1, -3),
+    ("L", 0, 1, 3), ("S", 0, 1, -3), ("S", 0, -1, 3), ("S", 0, 1, 3), ("pair", -1, 1), ("L", 1, -1, 4),
+    ("R", 0, -1, -2), ("R", 0, -1, 2), ("L", 1, 1, 4), ("R", 0, 2, 1), ("pair", 1, 1), ("L", 0, 2, -3),
+    ("S", 0, 2, -3), ("L", 1, 2, 3), ("R", 1, 2, -1), ("R", 1, -1, -2), ("R", 0, 2, -1), ("L", 0, 2, 3),
+    ("R", 1, 2, 1), ("S", 0, 2, 3), ("R", 1, -1, 2), ("R", 0, 1, -2), ("R", 1, 1, -2), ("R", 0, 1, 2),
+    ("pair", -1, -1), ("R", 0, 0, -3), ("R", 1, 1, 2), ("R", 0, 0, 3), ("R", 1, 0, -3), ("R", 1, 0, 3),
+    ("L", 0, -1, 4), ("pair", 1, -1), ("R", 0, -1, 3), ("L", 0, 1, 4), ("S", 0, -1, 4), ("S", 0, 1, 4),
+    ("R", 0, 2, 2), ("pair", 2, 1), ("R", 0, -1, -3), ("L", 1, 2, 4), ("R", 1, 2, -2), ("L", 0, 2, 4),
+    ("pair", 2, -1), ("S", 0, 2, 4), ("R", 0, 1, 3), ("R", 0, 2, -2), ("R", 0, 1, -3), ("R", 1, 2, 2), ("R", 0, 0, 4),
+    ("pair", -1, 0), ("R", 1, 0, 4), ("R", 1, -1, -3), ("R", 1, 1, -3), ("R", 1, -1, 3), ("R", 1, 1, 3),
+    ("pair", 1, 0), ("R", 0, 2, 3), ("pair", 2, 0), ("R", 0, -1, 4), ("R", 0, 2, -3), ("R", 0, 1, 4), ("R", 1, -1, 4),
+    ("R", 1, 1, 4), ("R", 1, 2, -3), ("R", 1, 2, 3), ("R", 0, 2, 4), ("rhs", 0), ("R", 1, 2, 4), ("rhs", 1),
 ]
 
 
@@ -83,7 +82,8 @@
     return lax.broadcasted_iota(jnp.int32, shape, axis)
 
 
-def kernel(gram, inv, cross_h, down, removed, updated, rhs_out,
+def kernel(gram, inv, cross_h, down_h, removed_h, updated, rhs_out,
+           down, removed,
            gt, pt, m_ref, cross, lsrc, ssrc, lall, sall, lrow, srow, rh, rl, ch,
            c0nat, pack, yslot, fbuf, zslot, lost, hh, hl,
            g_sem, in_sem, o_sem, l_send, l_recv, s_send, s_recv, c_send, c_recv, x_send, x_recv,
@@ -131,7 +131,11 @@
     def _():
         for j in range(8):
             loads[j].start()
+    d_load = pltpu.make_async_copy(down_h, down, in_sem.at[3])
+    i_load = pltpu.make_async_copy(removed_h, removed, in_sem.at[4])
+    i_load.start()
     m_load.start()
+    d_load.start()
     x_load.start()
 
     barrier = pltpu.get_barrier_semaphore()
@@ -139,7 +143,6 @@
     others += [at_col(lax.rem(col + off, 8)) for off in range(1, 8)]
     for dev in others:
         pl.semaphore_signal(barrier, inc=1, device_id=dev, device_id_type=MESH)
-    pl.semaphore_wait(barrier, len(others))
 
     class Stream:
         def __init__(self, buf, send, recv, rows, moves):
@@ -197,12 +200,48 @@
         block = c0_part(8 * y, 8, col)
         return [remote(block, block, c_send.at[6 + a], c_recv.at[7 + n], device_of(a, 0)) for a in (1, 2, 3)]
 
-    @pl.when(y < 2)
-    def _():
-        c0load.wait()
-        for c in c0_z():
-            c.start()
-
+    def hand_out(c):
+        return [remote(lsrc.at[c], lall.at[mine], x_send.at[c - 1], x_recv.at[0], at_col(c)),
+                remote(ssrc.at[c], sall.at[mine], x_send.at[7 + c - 1], x_recv.at[1], at_col(c))]
+
+    eye = iota((64, 128), 0) == iota((64, 128), 1)
+
+    def factor_rows(first):
+        r0 = first * 64
+        parts = [split2(gt[j, r0:r0 + 128, :]) for j in range(8)]
+        hi = jnp.concatenate([p[0] for p in parts], axis=1)
+        lo = jnp.concatenate([p[1] for p in parts], axis=1)
+        both = jnp.concatenate([hi, lo], axis=0)
+        blocks = []
+        for n in range(4):
+            k = 256 * (n + 1)
+            d = dot(both[:, :k], m_ref[256 * n:256 * n + 256, :k], NT)
+            blocks.append(d[:128] + d[128:])
+        top = jnp.maximum(blocks[0], -blocks[0])
+        for b in blocks[1:]:
+            top = jnp.maximum(top, jnp.abs(b))
+        scale = jnp.maximum(jnp.max(top, axis=1, keepdims=True), 1e-30) / 32767.0
+        inverse = 1.0 / scale
+        for i in range(2):
+            c = first + i
+            rows = slice(64 * i, 64 * i + 64)
+            for n in range(4):
+                q = lax.round(blocks[n][rows] * inverse[rows], lax.RoundingMethod.TO_NEAREST_EVEN)
+                q = jnp.clip(q, -32767.0, 32767.0).astype(jnp.int32).astype(I16)
+                half, lane = n // 2, 256 * (n % 2)
+                lsrc[c, 64 * half:64 * half + 64, lane:lane + 256] = q
+            lanes = jnp.sum(jnp.where(eye, jnp.broadcast_to(scale[rows], (64, 128)), 0.0), axis=0, keepdims=True)
+            ssrc[c] = jnp.broadcast_to(lanes, (8, 128))
+
+    @pl.when(col == 0)
+    def _():
+        for j in range(8):
+            loads[j].wait()
+        m_load.wait()
+        factor_rows(6)
+        factor_rows(4)
+
+    i_load.wait()
     rem = removed[...]
     flat = jnp.concatenate([rem[i:i + 1, :] for i in range(8)], axis=1)
 
@@ -215,48 +254,30 @@
     place = jnp.where(iota((shard, 1024), 0) == flat - base, 1.0, 0.0).astype(BF16)
     order = jnp.where(iota((128, 1024), 1) - first_of(base) == iota((128, 1024), 0), 1.0, 0.0).astype(BF16)
     pick = dot(order, place, NT).astype(BF16)
+    d_load.wait()
     pack[...] = dot(pick, down[...], NN).astype(BF16)
+    pl.semaphore_wait(barrier, len(others))
+
+    @pl.when(col == 0)
+    def _():
+        for c in (6, 4, 7, 5):
+            for cp in hand_out(c):
+                cp.start()
+
+    @pl.when(y < 2)
+    def _():
+        c0load.wait()
+        for c in c0_z():
+            c.start()
+
     yslot[y] = pack[...]
     ph1 = many([remote(pack, yslot.at[y], p_send.at[a - 1], p_recv.at[a - 1], device_of(a, 0)) for a in (1, 2, 3)])
 
-    def hand_out(c):
-        return [remote(lsrc.at[c], lall.at[mine], x_send.at[c - 1], x_recv.at[0], at_col(c)),
-                remote(ssrc.at[c], sall.at[mine], x_send.at[7 + c - 1], x_recv.at[1], at_col(c))]
-
-    eye = iota((64, 128), 0) == iota((64, 128), 1)
-
     @pl.when(col == 0)
     def _():
-        for j in range(8):
-            loads[j].wait()
-        m_load.wait()
-        for first in (4, 0):
-            r0 = first * 64
-            parts = [split2(gt[j, r0:r0 + 256, :]) for j in range(8)]
-            hi = jnp.concatenate([p[0] for p in parts], axis=1)
-            lo = jnp.concatenate([p[1] for p in parts], axis=1)
-            both = jnp.concatenate([hi, lo], axis=0)
-            blocks = []
-            for n in range(4):
-                k = 256 * (n + 1)
-                d = dot(both[:, :k], m_ref[256 * n:256 * n + 256, :k], NT)
-                blocks.append(d[:256] + d[256:])
-            top = jnp.maximum(blocks[0], -blocks[0])
-            for b in blocks[1:]:
-                top = jnp.maximum(top, jnp.abs(b))
-            scale = jnp.maximum(jnp.max(top, axis=1, keepdims=True), 1e-30) / 32767.0
-            inverse = 1.0 / scale
-            for i in range(4):
-                c = first + i
-                rows = slice(64 * i, 64 * i + 64)
-                for n in range(4):
-                    q = lax.round(blocks[n][rows] * inverse[rows], lax.RoundingMethod.TO_NEAREST_EVEN)
-                    q = jnp.clip(q, -32767.0, 32767.0).astype(jnp.int32).astype(I16)
-                    half, lane = n // 2, 256 * (n % 2)
-                    lsrc[c, 64 * half:64 * half + 64, lane:lane + 256] = q
-                lanes = jnp.sum(jnp.where(eye, jnp.broadcast_to(scale[rows], (64, 128)), 0.0), axis=0, keepdims=True)
-                ssrc[c] = jnp.broadcast_to(lanes, (8, 128))
-            for c in ((4, 6, 5, 7) if first == 4 else (2, 3, 1)):
+        for first in (2, 0):
+            factor_rows(first)
+            for c in range(max(first, 1), first + 2):
                 for cp in hand_out(c):
                     cp.start()
 
@@ -356,19 +377,17 @@
         cp.start()
         outs.append(cp)
 
-    def right_side():
-        for c in state["sc"]:
-            c.wait_recv()
-        x_load.wait()
-        r_hi, r_lo = split2(dot(c0nat[...].reshape(1024, 1024), lost[...].reshape(1024, 512), NN))
+    def right_side(part):
+        lanes = slice(256 * part, 256 * part + 256)
+        r_hi, r_lo = split2(dot(c0nat[...].reshape(1024, 1024), lost[:, :, lanes].reshape(1024, 256), NN))
         for n in range(4):
             k = 256 * (n + 1)
             mm = m_ref[256 * n:256 * n + 256, :k]
             hi, lo = split2(dot(mm, r_hi[:k], NN) + dot(mm, r_lo[:k], NN))
             hh[256 * n:256 * n + 256, :] = hi
             hl[256 * n:256 * n + 256, :] = lo
-        rhs = dot(cross[...], lost[...].reshape(1024, 512), NN)
-        rhs_out[...] = rhs - (dot(rh[...], hh[...], NN) + dot(rh[...], hl[...], NN) + dot(rl[...], hh[...], NN))
+        rhs = dot(cross[...], lost[:, :, lanes].reshape(1024, 256), NN)
+        rhs_out[:, lanes] = rhs - (dot(rh[...], hh[...], NN) + dot(rh[...], hl[...], NN) + dot(rl[...], hh[...], NN))
 
     def c0_across():
         @pl.when(y < 2)
@@ -411,15 +430,17 @@
         "C1": c0_across,
         "C2": c0_done,
         "CX": c0_forward,
+        "CW": lambda: ([c.wait_recv() for c in state["sc"]], x_load.wait()),
         "X": lambda: (forward_rows(1, "xs", "ss", srow), forward_rows(0, "xl", "sl", lrow)),
         "rows": lambda: (loaded(), rows_ready()),
-        "rhs": right_side,
-    }
+            }
     pairs = 0
     for event in ORDER:
         if event[0] in streams:
             wait_for(streams[event[0]], event[1:])
             start_from(streams[event[0]], event[1:])
+        elif event[0] == "rhs":
+            right_side(event[1])
         elif event[0] == "pair":
             columns(pairs, event[1], event[2])
             pairs += 1
@@ -451,19 +472,20 @@
     updated, rhs = pl.pallas_call(
         kernel,
         out_shape=[jax.ShapeDtypeStruct((512, 16, 128), F32), jax.ShapeDtypeStruct((512, 512), F32)],
-        in_specs=[hbm, hbm, hbm, vm, vm],
+        in_specs=[hbm] * 5,
         out_specs=[hbm, vm],
         scratch_shapes=[
-            v((8, 512, 128), F32), v((16, 512, 128), F32), v((1024, 1024), BF16), v((512, 1024), BF16),
+            v(down_rows.shape, BF16), v((8, 128), jnp.int32), v((8, 512, 128), F32), v((16, 512, 128), F32), v((1024, 1024), BF16), v((512, 1024), BF16),
             v((8, 128, 512), I16), v((8, 8, 128), F32), v((32, 128, 512), I16), v((32, 8, 128), F32),
             v((8, 128, 512), I16), v((8, 8, 128), F32), v((512, 1024), BF16), v((512, 1024), BF16),
             v((256, 1024), BF16),
             v((16, 4, 16, 1024), BF16), v((128, 512), BF16), v((4, 128, 512), BF16),
             v((8, 32, 512), BF16), v((8, 32, 512), BF16), v((32, 32, 512), BF16),
-            v((1024, 512), BF16), v((1024, 512), BF16),
-            dma((8,)), dma((3,)), dma((16,)), dma((big,)), dma((big,)), dma((small,)), dma((small,)),
+            v((1024, 256), BF16), v((1024, 256), BF16),
+            dma((8,)), dma((5,)), dma((16,)), dma((big,)), dma((big,)), dma((small,)), dma((small,)),
             dma((10,)), dma((9,)), dma((35,)), dma((23,)), dma((10,)), dma((10,)), dma((big,)), dma((big,)),
         ],
+        cost_estimate=pl.CostEstimate(flops=15_000_000_000, bytes_accessed=13_000_000, transcendentals=0),
         compiler_params=pltpu.CompilerParams(collective_id=0, has_side_effects=True, vmem_limit_bytes=56 << 20),
     )(gram.reshape(512, 16, 128), inv_factor, cross_gram.reshape(512, 1024), down_rows, removed.reshape(8, 128))
     updated = gram.reshape(512, 16, 128) - updated

time: 85.1 us -> 83.6 us (0.982)
  Pallas kernels: 78.2 us -> 76.5 us
    pallas_call x1, Pallas kernels: 78.2 us -> 76.5 us  [per_device(): pl.pallas_call(kernel, out_shape=[jax.ShapeDtypeStruct((512, 16, 128), F3...]
where the time goes in v3:
time: 83.6 us; the launch traced here: 83 us
  Pallas kernels  76.5 us (92%)
  other arithmetic  4.83 us (6%)
  local copies, waits for them, and re-layouts  0.98 us (1%)
    pallas_call x1, Pallas kernels, per_device(): pl.pallas_call(kernel, out_shape=[jax.ShapeDtypeStruct((512, 16, 128), F3...  76.5 us
    sub x1, other arithmetic, per_device(): updated = gram.reshape(512, 16, 128) - updated  4.83 us

profile of v3, /device:TPU:24, one launch (start us, length us, event | category | flops | bytes accessed | tf_op | source)
XLA Modules:
  0.0 83.0 jit_solution(18039180098676003383)
XLA Ops:
  0.6 0.0 copy-start
  0.6 76.5 %shard_map.68 = (f32[512,16,128]{2,1,0:T(8,128)}, f32[512,512]{1,0:T(8,128)}) custom-call(f32[512,16,128]{2,1,0:T(8,128)} %bitcast.7, bf16[1024,1024]{1,0:T(8,128)(2,1)} %inv.1, bf16[512,1024]{1,0:T(8,128)(2,1)} %bitcast.11, bf16[924,512]{1,0:T(8,128)(2,1)} %down_h.1, s32[8,128]{1,0:T(8,128)} %bitcast.12), custom_call_target="tpu_custom_call" | custom-call | flops 15000000512 | bytes 13000000 | tf_op jit(solution)/shard_map/pallas_call | solution.py:472
  77.2 0.0 copy-done
  77.2 0.0 copy-start.1
  77.2 4.8 %sub.3 = f32[512,16,128]{2,1,0:T(8,128)} subtract(f32[512,16,128]{2,1,0:T(8,128)S(1)} %bitcast.8, f32[512,16,128]{2,1,0:T(8,128)} %get-tuple-element.4) | non-fusion elementwise | flops 1048576 | bytes 12582912 | tf_op jit(solution)/shard_map/sub | solution.py:491
  82.0 0.0 copy-done.1
  82.0 1.0 %copy.10 = f32[8,1,64,512]{3,2,1,0:T(8,128)} copy(f32[8,1,64,512]{3,2,1,0:T(8,128)S(1)} %bitcast.10) | data formatting | bytes 2097152
Async XLA Ops:
  0.6 76.5 %copy-start = (f32[8,1,64,1,1,2048]{5,4,3,2,1,0:T(1,128)S(1)}, f32[8,1,64,1,1,2048]{5,4,3,2,1,0:T(1,128)}, u32[]{:S(2)}) copy-start(f32[8,1,64,1,1,2048]{5,4,3,2,1,0:T(1,128)} %param.5) | copy-start | bytes 12582916
  77.2 4.8 %copy-start.1 = (f32[512,512]{1,0:T(8,128)S(1)}, f32[512,512]{1,0:T(8,128)}, u32[]{:S(2)}) copy-start(f32[512,512]{1,0:T(8,128)} %get-tuple-element.5) | copy-start | bytes 3145732

commit v4 on v3

--- a/solution.py
+++ b/solution.py
@@ -38,34 +38,35 @@
 
 
 ORDER = [
-    ("own",), ("S", 0, 0, -1), ("S", 0, 0, 1), ("C1",), ("L", 1, 0, -1), ("L", 1, 0, 1), ("F",), ("L", 0, 0, -1),
-    ("X",), ("L", 0, 0, 1), ("S", 0, 0, -2), ("L", 0, -1, 0), ("S", 0, 0, 2), ("L", 0, 1, 0), ("L", 1, -1, 0),
-    ("L", 1, 1, 0), ("S", 0, -1, 0), ("S", 0, 1, 0), ("rows",), ("L", 1, 0, -2), ("L", 1, 0, 2), ("C2",),
+    ("own",), ("C1",), ("S", 0, 0, -1), ("S", 0, 0, 1), ("L", 1, 0, -1), ("L", 1, 0, 1), ("F",), ("L", 0, -1, 0),
+    ("L", 0, 1, 0), ("L", 0, 0, -1), ("L", 0, 0, 1), ("X",), ("S", 0, 0, -2), ("S", 0, 0, 2), ("L", 1, -1, 0),
+    ("L", 1, 1, 0), ("S", 0, -1, 0), ("S", 0, 1, 0), ("L", 1, 0, -2), ("L", 1, 0, 2), ("rows",), ("C2",),
     ("L", 1, -1, -1), ("L", 1, 1, -1), ("L", 1, -1, 1), ("L", 1, 1, 1), ("L", 0, 2, 0), ("L", 1, 2, 0),
-    ("S", 0, 2, 0), ("L", 0, 0, -2), ("S", 0, 0, -3), ("L", 0, 0, 2), ("pair", 0, 2), ("Rsum",), ("L", 0, -1, -1),
-    ("L", 0, -1, 1), ("L", 1, 1, -2), ("S", 0, 0, 3), ("L", 1, -1, -2), ("L", 0, 1, -1), ("S", 0, -1, -1),
-    ("S", 0, 1, -1), ("L", 0, 1, 1), ("S", 0, -1, 1), ("S", 0, 1, 1), ("L", 1, 1, 2), ("L", 1, -1, 2),
-    ("L", 1, 2, -1), ("L", 1, 0, -3), ("L", 1, 0, 3), ("CX",), ("R", 0, -1, 0), ("L", 1, 2, 1), ("L", 0, 2, -1),
-    ("R", 1, -1, 0), ("S", 0, 2, -1), ("L", 0, 2, 1), ("S", 0, 2, 1), ("R", 0, 1, 0), ("R", 1, 1, 0), ("L", 0, 0, -3),
-    ("pair", 0, 1), ("S", 0, 0, 4), ("L", 0, 0, 3), ("R", 0, 0, -1), ("R", 0, 0, 1), ("L", 1, 2, -2), ("R", 1, 0, -1),
-    ("R", 1, 0, 1), ("pair", 0, -1), ("L", 1, 2, 2), ("L", 0, -1, -2), ("L", 0, -1, 2), ("L", 1, -1, -3),
-    ("L", 0, 1, -2), ("S", 0, -1, -2), ("L", 0, 1, 2), ("S", 0, 1, -2), ("S", 0, -1, 2), ("S", 0, 1, 2),
-    ("pair", -1, 2), ("L", 1, 1, -3), ("R", 0, -1, -1), ("pair", 1, 2), ("L", 1, 0, 4), ("L", 1, -1, 3),
-    ("R", 0, -1, 1), ("CW",), ("R", 1, -1, -1), ("L", 1, 1, 3), ("L", 0, 2, -2), ("S", 0, 2, -2), ("R", 1, -1, 1),
-    ("R", 0, 2, 0), ("R", 1, 2, 0), ("R", 0, 1, -1), ("L", 0, 2, 2), ("S", 0, 2, 2), ("pair", 2, 2), ("R", 1, 1, -1),
-    ("R", 0, 1, 1), ("R", 1, 1, 1), ("L", 0, 0, 4), ("R", 0, 0, -2), ("R", 0, 0, 2), ("pair", 0, 0), ("R", 1, 0, -2),
-    ("R", 1, 0, 2), ("L", 1, 2, -3), ("L", 0, -1, -3), ("L", 0, -1, 3), ("L", 0, 1, -3), ("S", 0, -1, -3),
-    ("L", 0, 1, 3), ("S", 0, 1, -3), ("S", 0, -1, 3), ("S", 0, 1, 3), ("pair", -1, 1), ("L", 1, -1, 4),
-    ("R", 0, -1, -2), ("R", 0, -1, 2), ("L", 1, 1, 4), ("R", 0, 2, 1), ("pair", 1, 1), ("L", 0, 2, -3),
-    ("S", 0, 2, -3), ("L", 1, 2, 3), ("R", 1, 2, -1), ("R", 1, -1, -2), ("R", 0, 2, -1), ("L", 0, 2, 3),
-    ("R", 1, 2, 1), ("S", 0, 2, 3), ("R", 1, -1, 2), ("R", 0, 1, -2), ("R", 1, 1, -2), ("R", 0, 1, 2),
-    ("pair", -1, -1), ("R", 0, 0, -3), ("R", 1, 1, 2), ("R", 0, 0, 3), ("R", 1, 0, -3), ("R", 1, 0, 3),
-    ("L", 0, -1, 4), ("pair", 1, -1), ("R", 0, -1, 3), ("L", 0, 1, 4), ("S", 0, -1, 4), ("S", 0, 1, 4),
-    ("R", 0, 2, 2), ("pair", 2, 1), ("R", 0, -1, -3), ("L", 1, 2, 4), ("R", 1, 2, -2), ("L", 0, 2, 4),
-    ("pair", 2, -1), ("S", 0, 2, 4), ("R", 0, 1, 3), ("R", 0, 2, -2), ("R", 0, 1, -3), ("R", 1, 2, 2), ("R", 0, 0, 4),
-    ("pair", -1, 0), ("R", 1, 0, 4), ("R", 1, -1, -3), ("R", 1, 1, -3), ("R", 1, -1, 3), ("R", 1, 1, 3),
-    ("pair", 1, 0), ("R", 0, 2, 3), ("pair", 2, 0), ("R", 0, -1, 4), ("R", 0, 2, -3), ("R", 0, 1, 4), ("R", 1, -1, 4),
-    ("R", 1, 1, 4), ("R", 1, 2, -3), ("R", 1, 2, 3), ("R", 0, 2, 4), ("rhs", 0), ("R", 1, 2, 4), ("rhs", 1),
+    ("S", 0, 2, 0), ("L", 0, -1, -1), ("L", 0, -1, 1), ("L", 1, 1, -2), ("L", 1, -1, -2), ("L", 0, 1, -1),
+    ("L", 0, 1, 1), ("Rsum",), ("L", 1, 1, 2), ("L", 1, -1, 2), ("L", 0, 0, -2), ("S", 0, 0, -3), ("S", 0, -1, -1),
+    ("L", 0, 0, 2), ("S", 0, 1, -1), ("S", 0, 0, 3), ("S", 0, -1, 1), ("S", 0, 1, 1), ("pair", 0, 2), ("L", 1, 2, -1),
+    ("L", 1, 2, 1), ("L", 1, 0, -3), ("L", 1, 0, 3), ("L", 1, 2, -2), ("L", 0, 2, -1), ("S", 0, 2, -1),
+    ("R", 0, -1, 0), ("L", 0, 2, 1), ("S", 0, 2, 1), ("R", 0, 1, 0), ("R", 1, -1, 0), ("R", 1, 1, 0),
+    ("L", 0, -1, -2), ("L", 0, -1, 2), ("CX",), ("L", 1, 2, 2), ("L", 0, 1, -2), ("L", 0, 1, 2), ("R", 0, 0, -1),
+    ("R", 0, 0, 1), ("R", 1, 0, -1), ("R", 1, 0, 1), ("L", 0, 0, -3), ("pair", 0, 1), ("S", 0, 0, 4),
+    ("L", 1, -1, -3), ("S", 0, -1, -2), ("L", 0, 0, 3), ("L", 1, 1, -3), ("S", 0, 1, -2), ("S", 0, -1, 2),
+    ("S", 0, 1, 2), ("L", 1, 0, 4), ("pair", 0, -1), ("R", 0, -1, 1), ("L", 1, -1, 3), ("L", 1, 1, 3),
+    ("L", 0, 2, -2), ("S", 0, 2, -2), ("R", 0, 2, 0), ("R", 1, 2, 0), ("R", 0, -1, -1), ("R", 1, -1, -1),
+    ("R", 1, 1, -1), ("R", 0, 1, -1), ("L", 0, 2, 2), ("S", 0, 2, 2), ("R", 1, -1, 1), ("R", 1, 1, 1), ("R", 0, 1, 1),
+    ("pair", -1, 2), ("L", 0, -1, -3), ("L", 0, -1, 3), ("pair", 1, 2), ("L", 0, 1, -3), ("CW",), ("R", 0, 0, -2),
+    ("L", 0, 1, 3), ("L", 1, 2, -3), ("R", 1, 0, -2), ("R", 0, 0, 2), ("R", 1, 0, 2), ("pair", 2, 2),
+    ("S", 0, -1, -3), ("L", 0, 0, 4), ("S", 0, 1, -3), ("S", 0, -1, 3), ("S", 0, 1, 3), ("L", 1, -1, 4),
+    ("R", 0, -1, 2), ("R", 0, 2, 1), ("L", 1, 1, 4), ("L", 0, 2, -3), ("S", 0, 2, -3), ("pair", -1, 1),
+    ("R", 0, 2, -1), ("R", 0, -1, -2), ("L", 0, 2, 3), ("L", 1, 2, 3), ("S", 0, 2, 3), ("R", 1, 2, -1),
+    ("R", 0, 1, -2), ("R", 1, 2, 1), ("R", 0, 1, 2), ("pair", 0, 0), ("L", 0, -1, 4), ("R", 1, -1, -2),
+    ("R", 1, 1, -2), ("R", 0, 0, 3), ("R", 1, -1, 2), ("R", 1, 1, 2), ("L", 0, 1, 4), ("R", 1, 0, 3), ("R", 0, 0, -3),
+    ("pair", 1, 1), ("R", 1, 0, -3), ("S", 0, -1, 4), ("S", 0, 1, 4), ("R", 0, -1, 3), ("R", 0, 2, 2), ("S", 0, 2, 4),
+    ("pair", -1, -1), ("L", 1, 2, 4), ("R", 0, 2, -2), ("L", 0, 2, 4), ("R", 0, -1, -3), ("R", 0, 1, 3),
+    ("pair", 1, -1), ("R", 0, 1, -3), ("R", 1, 2, -2), ("R", 1, 2, 2), ("pair", 2, 1), ("R", 0, 0, 4),
+    ("R", 1, -1, 3), ("R", 1, 1, 3), ("R", 1, 0, 4), ("pair", 2, -1), ("R", 1, -1, -3), ("R", 1, 1, -3),
+    ("R", 0, 2, 3), ("pair", -1, 0), ("R", 0, 2, -3), ("R", 0, -1, 4), ("pair", 1, 0), ("R", 0, 1, 4), ("pair", 2, 0),
+    ("R", 1, 2, 3), ("R", 1, -1, 4), ("R", 1, 1, 4), ("R", 1, 2, -3), ("R", 0, 2, 4), ("rhs", 0), ("R", 1, 2, 4),
+    ("rhs", 1),
 ]
 
 

time: 83.6 us -> 81.8 us (0.978)
  the two profiles are of different devices: /device:TPU:24 before, /device:TPU:3 now
where the time goes in v4:
time: 81.8 us
  Pallas kernels  75.3 us (92%)
  other arithmetic  4.83 us (6%)
  local copies, waits for them, and re-layouts  0.98 us (1%)
    pallas_call x1, Pallas kernels, per_device(): pl.pallas_call(kernel, out_shape=[jax.ShapeDtypeStruct((512, 16, 128), F3...  75.3 us
    sub x1, other arithmetic, per_device(): updated = gram.reshape(512, 16, 128) - updated  4.83 us

profile of v4, /device:TPU:3, one launch (start us, length us, event | category | flops | bytes accessed | tf_op | source)
XLA Modules:
  0.0 81.8 jit_solution(17818617625645525144)
XLA Ops:
  0.6 0.0 copy-start
  0.6 75.3 %shard_map.68 = (f32[512,16,128]{2,1,0:T(8,128)}, f32[512,512]{1,0:T(8,128)}) custom-call(f32[512,16,128]{2,1,0:T(8,128)} %bitcast.7, bf16[1024,1024]{1,0:T(8,128)(2,1)} %inv.1, bf16[512,1024]{1,0:T(8,128)(2,1)} %bitcast.11, bf16[924,512]{1,0:T(8,128)(2,1)} %down_h.1, s32[8,128]{1,0:T(8,128)} %bitcast.12), custom_call_target="tpu_custom_call" | custom-call | flops 15000000512 | bytes 13000000 | tf_op jit(solution)/shard_map/pallas_call | solution.py:473
  75.9 0.0 copy-done
  75.9 0.0 copy-start.1
  76.0 4.8 %sub.3 = f32[512,16,128]{2,1,0:T(8,128)} subtract(f32[512,16,128]{2,1,0:T(8,128)S(1)} %bitcast.8, f32[512,16,128]{2,1,0:T(8,128)} %get-tuple-element.4) | non-fusion elementwise | flops 1048576 | bytes 12582912 | tf_op jit(solution)/shard_map/sub | solution.py:492
  80.8 0.0 copy-done.1
  80.8 1.0 %copy.10 = f32[8,1,64,512]{3,2,1,0:T(8,128)} copy(f32[8,1,64,512]{3,2,1,0:T(8,128)S(1)} %bitcast.10) | data formatting | bytes 2097152
Async XLA Ops:
  0.6 75.3 %copy-start = (f32[8,1,64,1,1,2048]{5,4,3,2,1,0:T(1,128)S(1)}, f32[8,1,64,1,1,2048]{5,4,3,2,1,0:T(1,128)}, u32[]{:S(2)}) copy-start(f32[8,1,64,1,1,2048]{5,4,3,2,1,0:T(1,128)} %param.5) | copy-start | bytes 12582916
  75.9 4.8 %copy-start.1 = (f32[512,512]{1,0:T(8,128)S(1)}, f32[512,512]{1,0:T(8,128)}, u32[]{:S(2)}) copy-start(f32[512,512]{1,0:T(8,128)} %get-tuple-element.5) | copy-start | bytes 3145732
